TPU v7x, 128 devices: a whole 4x4x4 slice. The times are simulated.
128 devices in a mesh: grp: 8 (over y, core), scen: 16 (over z, x).
Axes of the slice: x: 4, y: 4, z: 4, core: 2. Of those that a mesh axis runs over, the one named last changes fastest.
Arguments:
- linv: bfloat16 [256, 2048, 2048], P(('grp', 'scen'))
- link: bfloat16 [256, 2048, 512], P(('grp', 'scen')), may hold values from -0.125 to 0.125
- residual_rows: bfloat16 [256, 2048], P(('grp', 'scen')), may hold values from -24 to 24
- active: int32 [256], P(('grp', 'scen')), may hold values from 512 to 2048
- owner: int32 [256], P(('grp', 'scen')), may hold values from 0 to 255, each once
- weights: float32 [256], replicated, may hold values from 0.01 to 0.1
- first_diag: float32 [512], replicated, may hold values from 1 to 10
- first_rhs: float32 [512], replicated, may hold values from -24 to 24
Outputs:
- step_first: float32 [512], replicated
- scenario_newton_step: float32 [256, 2048], P(('grp', 'scen'))
All inputs are finite; a program needn't handle non-finite values.
Results may differ from a plain program's by a relative error of at most 0.0075.
Values sent between devices are 32-bit elements; how exact they have to be, the bound alone decides.
No kernel may reach another device: no remote copies, remote signals or barrier semaphores. Data moves between devices by JAX's collectives and lax.ppermute only.
A program may use at most 128 MiB of HBM per device.

v0:
```python
import jax
import jax.numpy as jnp
from jax import lax
from jax.sharding import PartitionSpec as P

ITERS = 2


def split_up(shard, dim, count):
    dims = shard.shape
    parts = shard.reshape(*dims[:dim], count, dims[dim] // count, *dims[dim + 1 :])
    return jnp.moveaxis(parts, dim, 0)


def sent_and_summed(shard, axis, dim):
    count = lax.axis_size(axis)
    parts = lax.all_to_all(split_up(shard, dim, count), axis, 0, 0, tiled=True)
    return jnp.sum(parts, axis=0)


def sent_together(arrays, axis, dim, along):
    columns = [a.reshape(*a.shape[:along], -1) for a in arrays]
    both = jnp.concatenate(columns, axis=along)
    filled, at, gathered = (sent_and_summed(both, axis, dim), 0, [])
    for a, column in zip(arrays, columns):
        section = filled[..., at : at + column.shape[along]]
        gathered.append(section.reshape(*section.shape[:along], *a.shape[along:]))
        at += column.shape[along]
    return tuple(gathered)


def sent_to_all(shard, axis):
    count = lax.axis_size(axis)
    return lax.all_to_all(
        jnp.broadcast_to(shard[None], (count, *shard.shape)), axis, 0, 0, tiled=True
    )


def over_copies(shard, axis):
    return sent_to_all(shard, axis).sum(axis=0)


def packed_total(arrays, axis):
    ends = [0]
    for a in arrays:
        ends.append(ends[-1] + a.size)
    so_far = over_copies(jnp.concatenate([a.ravel() for a in arrays]), axis)
    return tuple((so_far[b:e].reshape(a.shape) for a, b, e in zip(arrays, ends, ends[1:])))


def in_order(parts, dim):
    parts = jnp.moveaxis(parts, 0, dim)
    dims = parts.shape
    return parts.reshape(*dims[:dim], dims[dim] * dims[dim + 1], *dims[dim + 2 :])


def collect_2(shard, axis, dim):
    return in_order(sent_to_all(shard, axis), dim)


def body(linv, link, residual_rows, active, owner, weights, first_diag, first_rhs):
    local_count, rows = (linv.shape[0], linv.shape[1])
    width = link.shape[2]
    entry_offsets = lax.broadcasted_iota(jnp.int32, (local_count, rows), 1)
    keep = entry_offsets < active[:, None]
    masked = jnp.where(keep[:, :, None], link, jnp.zeros_like(link))
    solved = jnp.einsum("smk,skp->smp", linv, masked, preferred_element_type=jnp.float32).astype(
        jnp.bfloat16
    )
    lifted = jnp.einsum(
        "smk,sk->sm", linv, residual_rows, preferred_element_type=jnp.float32
    ).astype(jnp.bfloat16)
    numbers = lax.broadcasted_iota(jnp.int32, (local_count, weights.shape[0]), 1)
    probs = jnp.sum(jnp.where(owner[:, None] == numbers, weights[None, :], 0.0), axis=1)
    gram = jnp.einsum("smp,smq->spq", solved, solved, preferred_element_type=jnp.float32)
    cross = jnp.einsum("sm,smp->sp", lifted, solved, preferred_element_type=jnp.float32)
    partial_schur = jnp.einsum("s,spq->pq", probs, gram)
    partial_coupling_product = jnp.einsum("s,sp->p", probs, cross)
    grouped = sent_together((partial_schur, partial_coupling_product), "scen", 0, 1)
    schur_share, cross_share = packed_total((grouped[0], grouped[1]), "grp")
    offset = lax.axis_index("scen") * schur_share.shape[0]

    def collect(piece):
        return collect_2(piece, "scen", 0)

    def totals(values):
        return packed_total((values[0], values[1]), "scen")

    share_rows = schur_share.shape[0]
    row_ids = offset + lax.broadcasted_iota(jnp.int32, (share_rows, width), 0)
    col_ids = lax.broadcasted_iota(jnp.int32, (share_rows, width), 1)
    diag_rows = jnp.where(row_ids == col_ids, first_diag[None, :], 0.0)
    schur_rows = schur_share + diag_rows
    vector = lax.dynamic_slice_in_dim(first_rhs, offset, share_rows) - cross_share

    def operate(share):
        return jnp.dot(schur_rows, collect(share), precision=lax.Precision.HIGHEST)

    iterate = jnp.zeros_like(vector)
    remain = vector
    image = operate(remain)
    norm_now, product = totals((jnp.sum(remain * remain), jnp.sum(remain * image)))
    alpha = norm_now / product
    direction, along = (remain, image)
    for step in range(ITERS):
        iterate = iterate + alpha * direction
        remain = remain - alpha * along
        if step + 1 < ITERS:
            image = operate(remain)
            norm_next, product = totals((jnp.sum(remain * remain), jnp.sum(remain * image)))
            ratio = norm_next / norm_now
            alpha = norm_next / (product - ratio * norm_next / alpha)
            direction = remain + ratio * direction
            along = image + ratio * along
            norm_now = norm_next
    step_first = collect(iterate)
    step_bf = step_first.astype(jnp.bfloat16)
    residue = lifted.astype(jnp.float32) - jnp.einsum(
        "smp,p->sm", solved, step_bf, preferred_element_type=jnp.float32
    )
    scenario_newton_step = jnp.einsum(
        "smk,sm->sk", linv, residue.astype(jnp.bfloat16), preferred_element_type=jnp.float32
    )
    return (step_first, scenario_newton_step)


def solution(mesh):
    placed = (
        P(("grp", "scen"), None, None),
        P(("grp", "scen"), None, None),
        P(("grp", "scen"), None),
        P(("grp", "scen")),
        P(("grp", "scen")),
        P(),
        P(),
        P(),
    )
    return jax.shard_map(
        body, mesh=mesh, in_specs=placed, out_specs=(P(), P(("grp", "scen"), None)), check_vma=False
    )
```

profile of v0, /device:TPU:0, one launch (start us, length us, event | category | flops | bytes accessed | tf_op | source)
XLA Modules:
  0.0 157.8 jit_solution(3057657249694531202)
XLA Ops:
  0.6 0.7 iota_compare_fusion.1
  1.4 8.1 %fusion.19 = bf16[2,1,2048]{2,1,0:T(2,128)(2,1)S(1)} fusion(bf16[2,2048,2048]{2,1,0:T(8,128)(2,1)} %param.8, bf16[2,2048,1]{1,0,2:T(2,128)(2,1)S(1)} %bitcast.84), kind=kOutput, calls=%fused_computation.31 | convolution fusion | flops 16777216 | bytes 16793600 | tf_op jit(solution)/shard_map/smk,sk->sm/dot_general | solution.py:70
  9.5 14.9 %fusion.5 = bf16[2,512,2048]{2,1,0:T(8,128)(2,1)S(1)} fusion(bf16[2,2048,2048]{2,1,0:T(8,128)(2,1)} %param.8, bf16[2,2048,512]{2,1,0:T(8,128)(2,1)} %param.9, pred[2,2048]{1,0:T(4,128)(4,1)S(1)} %iota_compare_fusion.1), kind=kOutput, calls=%fused_computation.5 | convolution fusion | flops 8594128896 | bytes 25169920 | tf_op jit(solution)/shard_map/smk,skp->smp/dot_general | solution.py:67
  24.4 3.3 %fusion.29 = bf16[2,512,512]{2,1,0:T(8,128)(2,1)} fusion(bf16[2,512,2048]{2,1,0:T(8,128)(2,1)S(1)} %fusion.5), kind=kOutput, calls=%fused_computation.53 | convolution fusion | flops 2147483648 | bytes 5242880 | tf_op jit(solution)/shard_map/smp,smq->spq/dot_general | solution.py:75
  27.7 1.2 fusion.17
  29.5 2.4 %fusion.9 = f32[1,16,32,512]{3,0,2,1:T(1,128)S(1)} fusion(bf16[16,32,512,2]{2,1,0,3:T(8,128)(2,1)} %bitcast.91, bf16[2]{0:T(256)(128)(2,1)S(1)} %fusion.22), kind=kOutput, calls=%fused_computation.7 | convolution fusion | flops 1048576 | bytes 2097156 | tf_op jit(solution)/shard_map/s,spq->pq/dot_general | solution.py:77
  32.2 27.9 %all_to_all.41 = f32[16,32,513]{2,1,0:T(8,128)S(1)} all-to-all(f32[16,32,513]{2,1,0:T(8,128)S(1)} %pad_maximum_fusion), channel_id=1, replica_groups=mesh['grp'=8,'scen'=16] {'scen'}, dimensions={0} | all-to-all | bytes 2101248 | tf_op jit(solution)/shard_map/all_to_all | solution.py:17
  60.3 1.1 broadcast_in_dim.50
  61.4 4.5 %all-to-all-start.1 = ((f32[8,1,16416]{2,1,0:T(1,128)}), f32[8,1,16416]{2,1,0:T(1,128)S(1)}, u32[]{:S(2)}, u32[]{:S(2)}) async-start(f32[8,1,16416]{2,1,0:T(1,128)} %broadcast_in_dim.50), calls=%async_computation.1 | async-start | bytes 1056768 | tf_op jit(solution)/shard_map/all_to_all | solution.py:34
  66.0 10.2 %all-to-all-done.1 = f32[8,1,16416]{2,1,0:T(1,128)S(1)} async-done(((f32[8,1,16416]{2,1,0:T(1,128)}), f32[8,1,16416]{2,1,0:T(1,128)S(1)}, u32[]{:S(2)}, u32[]{:S(2)}) %all-to-all-start.1) | async-done | bytes 525344 | tf_op jit(solution)/shard_map/all_to_all | solution.py:34
  76.6 0.8 slice_subtract_fusion
  77.4 0.6 broadcast_in_dim.83
  78.0 3.5 %all-to-all-start.2 = ((f32[16,1,32]{2,1,0:T(1,128)}), f32[16,1,32]{2,1,0:T(1,128)S(1)}, u32[]{:S(2)}, u32[]{:S(2)}) async-start(f32[16,1,32]{2,1,0:T(1,128)} %broadcast_in_dim.83), calls=%async_computation.2 | async-start | bytes 16384 | tf_op jit(solution)/shard_map/all_to_all | solution.py:34
  81.5 7.4 %all-to-all-done.2 = f32[16,1,32]{2,1,0:T(1,128)S(1)} async-done(((f32[16,1,32]{2,1,0:T(1,128)}), f32[16,1,32]{2,1,0:T(1,128)S(1)}, u32[]{:S(2)}, u32[]{:S(2)}) %all-to-all-start.2) | async-done | bytes 2080 | tf_op jit(solution)/shard_map/all_to_all | solution.py:34
  88.9 0.5 broadcast.90
  89.4 0.7 reduce.14
  90.2 0.8 multiply_reduce_fusion.2
  91.0 1.3 pad_maximum_fusion.2
  92.3 10.6 %all_to_all.42 = f32[16,1,2]{2,1,0:T(1,128)S(1)} all-to-all(f32[16,1,2]{2,1,0:T(1,128)S(1)} %broadcast_in_dim.84), channel_id=1, replica_groups=mesh['grp'=8,'scen'=16] {'scen'}, dimensions={0} | all-to-all | bytes 256 | tf_op jit(solution)/shard_map/all_to_all | solution.py:34
  102.9 0.6 fusion.28
  104.8 0.6 multiply_reduce_fusion
  105.5 10.6 %all_to_all.43 = f32[16,1,32]{2,1,0:T(1,128)S(1)} all-to-all(f32[16,1,32]{2,1,0:T(1,128)S(1)} %broadcast_in_dim.85), channel_id=1, replica_groups=mesh['grp'=8,'scen'=16] {'scen'}, dimensions={0} | all-to-all | bytes 4096 | tf_op jit(solution)/shard_map/all_to_all | solution.py:34
  116.0 0.7 reduce.15
  116.8 0.8 fusion.12
  117.6 1.4 pad_maximum_fusion.3
  119.0 10.6 %all_to_all.44 = f32[16,1,2]{2,1,0:T(1,128)S(1)} all-to-all(f32[16,1,2]{2,1,0:T(1,128)S(1)} %broadcast_in_dim.86), channel_id=1, replica_groups=mesh['grp'=8,'scen'=16] {'scen'}, dimensions={0} | all-to-all | bytes 256 | tf_op jit(solution)/shard_map/all_to_all | solution.py:34
  129.6 0.6 fusion.27
  134.9 10.6 %all_to_all.45 = f32[16,1,32]{2,1,0:T(1,128)S(1)} all-to-all(f32[16,1,32]{2,1,0:T(1,128)S(1)} %broadcast_in_dim.87), channel_id=1, replica_groups=mesh['grp'=8,'scen'=16] {'scen'}, dimensions={0} | all-to-all | bytes 4096 | tf_op jit(solution)/shard_map/all_to_all | solution.py:34
  145.5 0.7 reduce.16
  146.2 2.8 %fusion = f32[1,2,2048]{2,0,1:T(1,128)S(1)} fusion(bf16[512,1,1]{0,1,2:T(2,128)(2,1)S(1)} %reshape.181, bf16[2,512,2048]{2,1,0:T(8,128)(2,1)} %copy-done.1), kind=kOutput, calls=%fused_computation | convolution fusion | flops 4194304 | bytes 4211712 | tf_op jit(solution)/shard_map/smp,p->sm/dot_general | solution.py:118
  149.1 8.0 %fusion.14 = f32[2,1,2048]{2,1,0:T(1,128)S(1)} fusion(bf16[2,2048,2048]{2,1,0:T(8,128)(2,1)} %param.8, bf16[2,2048,1]{1,0,2:T(2,128)(2,1)S(1)} %fusion.21), kind=kOutput, calls=%fused_computation.26 | convolution fusion | flops 16777216 | bytes 16801792 | tf_op jit(solution)/shard_map/smk,sm->sk/dot_general | solution.py:121
  157.1 0.6 copy.69
  (43 shorter events, 1.9 us)
Async XLA Ops:
  0.6 0.8 copy-start
  24.4 3.4 %copy-start.1 = (bf16[2,512,2048]{2,1,0:T(8,128)(2,1)}, bf16[2,512,2048]{2,1,0:T(8,128)(2,1)S(1)}, u32[]{:S(2)}) copy-start(bf16[2,512,2048]{2,1,0:T(8,128)(2,1)S(1)} %fusion.5) | copy-start | bytes 12582916
  27.7 1.3 copy-start.4
  27.7 1.3 copy-start.5
  32.0 33.9 %copy-start.3 = (f32[512]{0:T(512)S(1)}, f32[512]{0:T(512)}, u32[]{:S(2)}) copy-start(f32[512]{0:T(512)} %param.14) | copy-start | bytes 6148
  61.4 14.8 %all-to-all-start.1 = ((f32[8,1,16416]{2,1,0:T(1,128)}), f32[8,1,16416]{2,1,0:T(1,128)S(1)}, u32[]{:S(2)}, u32[]{:S(2)}) async-start(f32[8,1,16416]{2,1,0:T(1,128)} %broadcast_in_dim.50), calls=%async_computation.1 | async-start | bytes 1056768 | tf_op jit(solution)/shard_map/all_to_all | solution.py:34
  78.0 10.9 %all-to-all-start.2 = ((f32[16,1,32]{2,1,0:T(1,128)}), f32[16,1,32]{2,1,0:T(1,128)S(1)}, u32[]{:S(2)}, u32[]{:S(2)}) async-start(f32[16,1,32]{2,1,0:T(1,128)} %broadcast_in_dim.83), calls=%async_computation.2 | async-start | bytes 16384 | tf_op jit(solution)/shard_map/all_to_all | solution.py:34
  146.2 10.9 %copy-start.2 = (f32[512]{0:T(512)}, f32[512]{0:T(512)S(1)}, u32[]{:S(2)}) copy-start(f32[512]{0:T(512)S(1)} %reshape.168) | copy-start | bytes 6148
where the time goes:
time: 159 us; the launch traced here: 158 us
  blocking collectives  70.2 us (44%)
  matrix products  42.7 us (27%)
  waiting for transfers between devices  17.7 us (11%)
  starting transfers between devices  7.95 us (5%)
  other arithmetic  7.81 us (5%)
  between operations  6.8 us (4%)
  local copies, waits for them, and re-layouts  4.69 us (3%)
    all_to_all x4, blocking collectives, sent_to_all(): lax.all_to_all(jnp.broadcast_to(shard[None], (count, *shard.shape)), axis...  42.3 us
    all_to_all x1, blocking collectives, sent_and_summed(): parts = lax.all_to_all(split_up(shard, dim, count), axis, 0, 0, tiled=True)  27.9 us
    all_to_all x2, waiting for transfers between devices, sent_to_all(): lax.all_to_all(jnp.broadcast_to(shard[None], (count, *shard.shape)), axis...  17.7 us
    dot_general x1, matrix products, body(): jnp.einsum('smk,skp->smp', linv, masked, preferred_element_type=jnp.float32)  14.9 us
    dot_general x1, matrix products, body(): jnp.einsum('smk,sk->sm', linv, residual_rows, preferred_element_type=jnp....  8.05 us
    dot_general x1, matrix products, body(): jnp.einsum('smk,sm->sk', linv, residue.astype(jnp.bfloat16), preferred_el...  8.04 us
    all_to_all x2, starting transfers between devices, sent_to_all(): lax.all_to_all(jnp.broadcast_to(shard[None], (count, *shard.shape)), axis...  7.95 us
    dot_general x1, matrix products, body(): jnp.einsum('smp,smq->spq', solved, solved, preferred_element_type=jnp.flo...  3.34 us
  transfers between devices with their start and end apart: 2, of which 2 were waited for; matrix products, arithmetic and copies ran while one was open for 0% of the time, Pallas kernels for 0%

commit v1 on v0

v1 whole, which is shorter than its diff:
```python
import jax
import jax.numpy as jnp
from jax import lax
from jax.experimental import pallas as pl
from jax.experimental.pallas import tpu as pltpu
from jax.sharding import PartitionSpec as P

BOTH = ("grp", "scen")
BLOCK = 256
NT = (((1,), (1,)), ((), ()))
NN = (((1,), (0,)), ((), ()))
TN = (((0,), (0,)), ((), ()))
VMEM_LIMIT = 56 * 1024 * 1024
SMEM_SPEC = pl.BlockSpec(memory_space=pltpu.SMEM)
VMEM_SPEC = pl.BlockSpec(memory_space=pltpu.VMEM)
ANY_SPEC = pl.BlockSpec(memory_space=pl.ANY)


def mul(a, b, dims):
    return lax.dot_general(a, b, dims, preferred_element_type=jnp.float32)


def pieces(row):
    high = row.astype(jnp.bfloat16).astype(jnp.float32)
    rest = row - high
    middle = rest.astype(jnp.bfloat16).astype(jnp.float32)
    low = rest - middle
    width = row.shape[1]
    ids = lax.broadcasted_iota(jnp.int32, (8, width), 0)
    spread = lambda part: jnp.broadcast_to(part, (8, width))
    out = jnp.where(ids == 0, spread(high), jnp.where(ids == 1, spread(middle), jnp.where(ids == 2, spread(low), 0.0)))
    return out.astype(jnp.bfloat16)


def total(rows):
    return jnp.sum(rows, axis=0, keepdims=True)


def block_copies(linv, buffer, sems, count, blocks):
    copies = []
    for s in range(count):
        for i in range(blocks):
            where = (s, pl.ds(i * BLOCK, BLOCK), pl.ds(0, (i + 1) * BLOCK))
            copies.append(pltpu.make_async_copy(linv.at[where], buffer.at[where], sems.at[s, i]))
    return copies


def first_kernel(owner, weights, active, linv, link, right, lift_out, cross_out, lbuf, kbuf, acc, sems, link_sems):
    count, rows, width = link.shape
    blocks = rows // BLOCK
    copies = block_copies(linv, lbuf, sems, count, blocks)
    for copy in copies:
        copy.start()
    links = [pltpu.make_async_copy(link.at[s], kbuf.at[s], link_sems.at[s]) for s in range(count)]
    for copy in links:
        copy.start()
    cross = jnp.zeros((1, width), jnp.float32)
    products = []
    for s in range(count):
        wide = jnp.broadcast_to(right[s].astype(jnp.float32), (8, rows)).astype(jnp.bfloat16)
        acc[s] = jnp.zeros((8, rows), jnp.float32)
        for i in range(blocks):
            copies[s * blocks + i].wait()
            span = (i + 1) * BLOCK
            tile = lbuf[s, pl.ds(i * BLOCK, BLOCK), pl.ds(0, span)]
            lifted = mul(wide[:, :span], tile, NT).astype(jnp.bfloat16)
            acc[s, :, pl.ds(0, span)] += mul(lifted, tile, NN)
        product = acc[s, pl.ds(0, 1), :]
        lift_out[s] = product
        products.append(product)
    ids = lax.broadcasted_iota(jnp.int32, (1, rows), 1)
    for s in range(count):
        links[s].wait()
        kept = jnp.where(ids < active[s], products[s], 0.0)
        cross = cross + weights[owner[s]] * total(mul(pieces(kept), kbuf[s], NN))
    cross_out[...] = jnp.broadcast_to(cross, cross_out.shape)


def gram_kernel(owner, weights, active, linv, link, solved_out, gram_out, lbuf, kbuf, sems, link_sems):
    count, rows, width = link.shape
    blocks = rows // BLOCK
    copies = block_copies(linv, lbuf, sems, count, blocks)
    links = []
    for s in range(count):
        for i in range(blocks):
            where = (s, pl.ds(i * BLOCK, BLOCK))
            links.append(pltpu.make_async_copy(link.at[where], kbuf.at[where], link_sems.at[s, i]))
    for a, b in zip(links, copies):
        a.start()
        b.start()
    for s in range(count):
        for i in range(blocks):
            links[s * blocks + i].wait()
            ids = i * BLOCK + lax.broadcasted_iota(jnp.int32, (BLOCK, width), 0)
            part = kbuf[s, pl.ds(i * BLOCK, BLOCK)]
            kbuf[s, pl.ds(i * BLOCK, BLOCK)] = jnp.where(ids < active[s], part, jnp.zeros_like(part))
            copies[s * blocks + i].wait()
            span = (i + 1) * BLOCK
            tile = lbuf[s, pl.ds(i * BLOCK, BLOCK), pl.ds(0, span)]
            solved_out[s, pl.ds(i * BLOCK, BLOCK)] = mul(tile, kbuf[s, pl.ds(0, span)], NN).astype(jnp.bfloat16)
        gram = weights[owner[s]] * mul(solved_out[s], solved_out[s], TN)
        if s == 0:
            gram_out[...] = gram
        else:
            gram_out[...] += gram


def exact_mul(row, matrix):
    wide = jnp.broadcast_to(row, (8, row.shape[1]))
    return lax.dot_general(wide, matrix, NN, precision=lax.Precision.HIGHEST, preferred_element_type=jnp.float32)[:1]


def image_kernel(parts, rhs, gram, vector_out, image_out):
    vector = rhs[...] - total(parts[...])
    vector_out[...] = vector
    image_out[...] = jnp.broadcast_to(exact_mul(vector, gram[...]), image_out.shape)


def direction_kernel(parts, diag, vector_in, gram, direction_out, scalars_out, product_out):
    vector = vector_in[...]
    image = diag[...] * vector + total(parts[...])
    dot = lambda a, b: jnp.sum(a * b, axis=1, keepdims=True)
    norm = dot(vector, vector)
    alpha = norm / dot(vector, image)
    remain = vector - alpha * image
    norm_next = dot(remain, remain)
    direction = remain + (norm_next / norm) * vector
    direction_out[...] = direction
    wide = lambda value: jnp.broadcast_to(value, (1, 128))
    scalars_out[pl.ds(0, 1)] = wide(alpha)
    scalars_out[pl.ds(1, 1)] = wide(norm_next)
    scalars_out[pl.ds(2, 1)] = wide(dot(direction * diag[...], direction))
    product_out[...] = jnp.broadcast_to(dot(exact_mul(direction, gram[...]), direction), product_out.shape)


def back_kernel(linv, solved, row, back_out, lbuf, acc, sems):
    count, rows, width = solved.shape
    blocks = rows // BLOCK
    copies = block_copies(linv, lbuf, sems, count, blocks)
    for copy in copies:
        copy.start()
    split = pieces(row[...])
    for s in range(count):
        acc[s] = jnp.zeros((8, rows), jnp.float32)
        for i in range(blocks):
            forward = total(mul(split, solved[s, pl.ds(i * BLOCK, BLOCK)], NT))
            spread = pieces(forward)
            copies[s * blocks + i].wait()
            span = (i + 1) * BLOCK
            tile = lbuf[s, pl.ds(i * BLOCK, BLOCK), pl.ds(0, span)]
            acc[s, :, pl.ds(0, span)] += mul(spread, tile, NN)
        back_out[s] = total(acc[s])


def last_kernel(parts, scalars, vector, direction, lift, first, second, step_out, out):
    alpha = scalars[pl.ds(0, 1), pl.ds(0, 1)]
    norm = scalars[pl.ds(1, 1), pl.ds(0, 1)]
    bend = total(parts[...])[:, :1] + scalars[pl.ds(2, 1), pl.ds(0, 1)]
    beta = norm / bend
    step_out[...] = alpha * vector[...] + beta * direction[...]
    for s in range(out.shape[0]):
        out[pl.ds(s, 1)] = lift[s] - alpha * first[s] - beta * second[s]


def params():
    return pltpu.CompilerParams(vmem_limit_bytes=VMEM_LIMIT)


def body(linv, link, residual_rows, active, owner, weights, first_diag, first_rhs):
    count, rows, width = link.shape
    blocks = rows // BLOCK
    devices = lax.axis_size(BOTH)
    f32 = lambda *dims: jax.ShapeDtypeStruct(dims, jnp.float32)
    l_scratch = pltpu.VMEM((count, rows, rows), jnp.bfloat16)
    k_scratch = pltpu.VMEM((count, rows, width), jnp.bfloat16)
    acc_scratch = pltpu.VMEM((count, 8, rows), jnp.float32)
    block_sems = pltpu.SemaphoreType.DMA((count, blocks))

    def share(rows_of_all):
        return lax.all_to_all(rows_of_all, BOTH, 0, 0, tiled=True)

    right = residual_rows.reshape(count, 1, rows)
    diag = first_diag.reshape(1, width)
    rhs = first_rhs.reshape(1, width)
    lift, cross = pl.pallas_call(
        first_kernel,
        name="first",
        out_shape=(f32(count, 1, rows), f32(devices, width)),
        in_specs=[SMEM_SPEC] * 3 + [ANY_SPEC] * 2 + [VMEM_SPEC],
        out_specs=(VMEM_SPEC, VMEM_SPEC),
        scratch_shapes=[l_scratch, k_scratch, acc_scratch, block_sems, pltpu.SemaphoreType.DMA((count,))],
        compiler_params=params(),
    )(owner, weights, active, linv, link, right)
    cross_parts = share(cross)
    solved, gram = pl.pallas_call(
        gram_kernel,
        name="gram",
        out_shape=(jax.ShapeDtypeStruct((count, rows, width), jnp.bfloat16), f32(width, width)),
        in_specs=[SMEM_SPEC] * 3 + [ANY_SPEC] * 2,
        out_specs=(VMEM_SPEC, VMEM_SPEC),
        scratch_shapes=[l_scratch, k_scratch, block_sems, block_sems],
        compiler_params=params(),
    )(owner, weights, active, linv, link)
    vector, image = pl.pallas_call(
        image_kernel, name="image", out_shape=(f32(1, width), f32(devices, width)), compiler_params=params()
    )(cross_parts, rhs, gram)
    image_parts = share(image)

    def back(row, name):
        return pl.pallas_call(
            back_kernel,
            name=name,
            out_shape=f32(count, 1, rows),
            in_specs=[ANY_SPEC, VMEM_SPEC, VMEM_SPEC],
            out_specs=VMEM_SPEC,
            scratch_shapes=[l_scratch, acc_scratch, block_sems],
            compiler_params=params(),
        )(linv, solved, row)

    first = back(vector, "back_first")
    direction, scalars, product = pl.pallas_call(
        direction_kernel,
        name="direction",
        out_shape=(f32(1, width), f32(3, 128), f32(devices, 128)),
        compiler_params=params(),
    )(image_parts, diag, vector, gram)
    product_parts = share(product)
    second = back(direction, "back_second")
    step, out = pl.pallas_call(
        last_kernel, name="last", out_shape=(f32(1, width), f32(count, rows)), compiler_params=params()
    )(product_parts, scalars, vector, direction, lift, first, second)
    return step.reshape(width), out


def solution(mesh):
    placed = (
        P(BOTH, None, None),
        P(BOTH, None, None),
        P(BOTH, None),
        P(BOTH),
        P(BOTH),
        P(),
        P(),
        P(),
    )
    return jax.shard_map(body, mesh=mesh, in_specs=placed, out_specs=(P(), P(BOTH, None)), check_vma=False)
```

time: 159 us -> 94.5 us (0.59)
  Pallas kernels: 0 us -> 50.3 us
  blocking collectives: 70.2 us -> 20.4 us
  matrix products: 42.7 us -> 0 us
  waiting for transfers between devices: 17.7 us -> 0.01 us
  starting transfers between devices: 7.95 us -> 15.8 us
  other arithmetic: 7.81 us -> 0 us
  between operations: 6.8 us -> 0.71 us
  local copies, waits for them, and re-layouts: 4.69 us -> 6.57 us
    pallas_call x0 -> x7, Pallas kernels: none -> 50.3 us  [the longest x2 18.6 us: back(): pl.pallas_call(back_kernel, name=name, out_shape=f32(count, 1, rows), in_...]
    all_to_all x5 -> x1, blocking collectives: 70.2 us -> 20.4 us  [share(): return lax.all_to_all(rows_of_all, BOTH, 0, 0, tiled=True)]
    dot_general x10 -> x0, matrix products: 42.7 us -> none  [the longest x1 14.9 us: body(): jnp.einsum('smk,skp->smp', linv, masked, preferred_element_type=jnp.float32)]
    all_to_all x2, waiting for transfers between devices: 17.7 us -> 0.01 us  [share(): return lax.all_to_all(rows_of_all, BOTH, 0, 0, tiled=True)]
    all_to_all x2, starting transfers between devices: 7.95 us -> 15.8 us  [share(): return lax.all_to_all(rows_of_all, BOTH, 0, 0, tiled=True)]
    concatenate x4 -> x0, other arithmetic: 2.83 us -> none  [the longest x3 2.71 us: packed_total(): so_far = over_copies(jnp.concatenate([a.ravel() for a in arrays]), axis)]
    all_to_all x1 -> x2, local copies, waits for them, and re-layouts: 0.51 us -> 3.16 us  [share(): return lax.all_to_all(rows_of_all, BOTH, 0, 0, tiled=True)]
    unnamed x15 -> x4, local copies, waits for them, and re-layouts: 0.08 us -> 2.09 us
  transfers between devices with their start and end apart: 2 -> 2, of which waited for: 2 -> 0; matrix products, arithmetic and copies ran while one was open for 0% -> 0% of each run, Pallas kernels for 0% -> 34%
where the time goes in v1:
time: 94.5 us; the launch traced here: 93.7 us
  Pallas kernels  50.3 us (53%)
  blocking collectives  20.4 us (22%)
  starting transfers between devices  15.8 us (17%)
  local copies, waits for them, and re-layouts  6.57 us (7%)
    all_to_all x1, blocking collectives, share(): return lax.all_to_all(rows_of_all, BOTH, 0, 0, tiled=True)  20.4 us
    pallas_call x2, Pallas kernels, back(): pl.pallas_call(back_kernel, name=name, out_shape=f32(count, 1, rows), in_...  18.6 us
    all_to_all x2, starting transfers between devices, share(): return lax.all_to_all(rows_of_all, BOTH, 0, 0, tiled=True)  15.8 us
    pallas_call x1, Pallas kernels, body(): pl.pallas_call(gram_kernel, name='gram', out_shape=(jax.ShapeDtypeStruct(...  13.4 us
    pallas_call x1, Pallas kernels, body(): pl.pallas_call(first_kernel, name='first', out_shape=(f32(count, 1, rows)...  11.2 us
    all_to_all x2, local copies, waits for them, and re-layouts, share(): return lax.all_to_all(rows_of_all, BOTH, 0, 0, tiled=True)  3.16 us
    pallas_call x1, Pallas kernels, body(): pl.pallas_call(direction_kernel, name='direction', out_shape=(f32(1, widt...  2.75 us
    pallas_call x1, Pallas kernels, body(): pl.pallas_call(image_kernel, name='image', out_shape=(f32(1, width), f32(...  2.64 us
  transfers between devices with their start and end apart: 2, of which 0 were waited for; matrix products, arithmetic and copies ran while one was open for 0% of the time, Pallas kernels for 34%

profile of v1, /device:TPU:0, one launch (start us, length us, event | category | flops | bytes accessed | tf_op | source)
XLA Modules:
  0.0 93.7 jit_solution(16651245072413934631)
XLA Ops:
  0.6 1.3 %copy.11.right = bf16[2,1,2048]{2,1,0:T(2,128)(2,1)} copy(bf16[2,1,2048]{2,0,1:T(2,128)(2,1)} %bitcast.22) | data formatting | bytes 16384 | tf_op jit(solution)/shard_map/reshape | solution.py:182
  1.9 11.2 %first.1 = (f32[2,1,2048]{2,1,0:T(1,128)}, f32[128,512]{1,0:T(8,128)}) custom-call(s32[2]{0:T(128)} %owner.3, f32[256]{0:T(256)} %weights.3, s32[2]{0:T(128)} %active.3, bf16[2,2048,2048]{2,1,0:T(8,128)(2,1)} %linv.7, bf16[2,2048,512]{2,1,0:T(8,128)(2,1)} %link.3, bf16[2,1,2048]{2,1,0:T(2,128)(2,1)} %copy.11.right), custom_call_target="tpu_custom_call" | custom-call | tf_op jit(solution)/shard_map/first/pallas_call | solution.py:185
  13.2 1.9 %copy.12 = f32[128,1,512]{2,1,0:T(1,128)} copy(f32[128,1,512]{2,0,1:T(8,128)} %bitcast.18) | data formatting | bytes 524288 | tf_op jit(solution)/shard_map/all_to_all | solution.py:180
  15.1 11.2 %all-to-all-start = ((f32[128,1,512]{2,1,0:T(1,128)}), f32[128,1,512]{2,1,0:T(1,128)S(1)}, u32[]{:S(2)}, u32[]{:S(2)}) async-start(f32[128,1,512]{2,1,0:T(1,128)} %copy.12), calls=%async_computation | async-start | bytes 524288 | tf_op jit(solution)/shard_map/all_to_all | solution.py:180
  26.3 13.4 %gram.1 = (bf16[2,2048,512]{2,1,0:T(8,128)(2,1)}, f32[512,512]{1,0:T(8,128)}) custom-call(s32[2]{0:T(128)} %owner.3, f32[256]{0:T(256)} %weights.3, s32[2]{0:T(128)} %active.3, bf16[2,2048,2048]{2,1,0:T(8,128)(2,1)} %linv.7, bf16[2,2048,512]{2,1,0:T(8,128)(2,1)} %link.3), custom_call_target="tpu_custom_call" | custom-call | tf_op jit(solution)/shard_map/gram/pallas_call | solution.py:195
  39.7 0.0 all-to-all-done
  39.7 0.7 copy.20
  40.5 2.6 %image.1 = (f32[1,512]{1,0:T(1,128)}, f32[128,512]{1,0:T(8,128)}) custom-call(f32[128,512]{1,0:T(8,128)} %bitcast.17, f32[1,512]{1,0:T(1,128)} %bitcast.23, f32[512,512]{1,0:T(8,128)} %get-tuple-element.14.gram), custom_call_target="tpu_custom_call" | custom-call | tf_op jit(solution)/shard_map/image/pallas_call | solution.py:204
  43.1 1.2 %copy.13 = f32[128,1,512]{2,1,0:T(1,128)S(1)} copy(f32[128,1,512]{2,0,1:T(8,128)} %bitcast.19) | data formatting | bytes 524288 | tf_op jit(solution)/shard_map/all_to_all | solution.py:180
  44.3 20.4 %all_to_all.33 = f32[128,1,512]{2,1,0:T(1,128)S(1)} all-to-all(f32[128,1,512]{2,1,0:T(1,128)S(1)} %copy.13), channel_id=1, replica_groups=mesh['grp'=8,'scen'=16] {'grp','scen'}, dimensions={0} | all-to-all | bytes 524288 | tf_op jit(solution)/shard_map/all_to_all | solution.py:180
  64.8 0.7 copy.19
  65.5 2.7 %direction.1 = (f32[1,512]{1,0:T(1,128)}, f32[3,128]{1,0:T(4,128)}, f32[128,128]{1,0:T(8,128)}) custom-call(f32[128,512]{1,0:T(8,128)} %bitcast.16, f32[1,512]{1,0:T(1,128)} %bitcast.24, f32[1,512]{1,0:T(1,128)} %get-tuple-element.16.vector_in.row.vector, f32[512,512]{1,0:T(8,128)} %get-tuple-element.14.gram), custom_call_target="tpu_custom_call" | custom-call | tf_op jit(solution)/shard_map/direction/pallas_call | solution.py:221
  68.2 4.6 %all-to-all-start.2 = ((f32[128,1,128]{2,1,0:T(1,128)}), f32[128,1,128]{2,1,0:T(1,128)S(1)}, u32[]{:S(2)}, u32[]{:S(2)}) async-start(f32[128,1,128]{2,1,0:T(1,128)} %bitcast.21), calls=%async_computation.2 | async-start | bytes 131072 | tf_op jit(solution)/shard_map/all_to_all | solution.py:180
  72.9 9.3 %back_first.1.first = f32[2,1,2048]{2,1,0:T(1,128)} custom-call(bf16[2,2048,2048]{2,1,0:T(8,128)(2,1)} %linv.7, bf16[2,2048,512]{2,1,0:T(8,128)(2,1)} %get-tuple-element.21.solved, f32[1,512]{1,0:T(1,128)} %get-tuple-element.16.vector_in.row.vector), custom_call_target="tpu_custom_call" | custom-call | tf_op jit(solution)/shard_map/back_first/pallas_call | solution.py:210
  82.2 9.3 %back_second.1.second = f32[2,1,2048]{2,1,0:T(1,128)} custom-call(bf16[2,2048,2048]{2,1,0:T(8,128)(2,1)} %linv.7, bf16[2,2048,512]{2,1,0:T(8,128)(2,1)} %get-tuple-element.21.solved, f32[1,512]{1,0:T(1,128)} %get-tuple-element.19.row.direction), custom_call_target="tpu_custom_call" | custom-call | tf_op jit(solution)/shard_map/back_second/pallas_call | solution.py:210
  91.5 0.0 all-to-all-done.2
  91.5 0.0 copy-start
  91.5 0.6 copy-done
  92.1 1.6 %last.1 = (f32[1,512]{1,0:T(1,128)}, f32[2,2048]{1,0:T(2,128)}) custom-call(f32[128,128]{1,0:T(8,128)} %bitcast.20, f32[3,128]{1,0:T(4,128)} %get-tuple-element.18.scalars, f32[1,512]{1,0:T(1,128)} %get-tuple-element.16.vector_in.row.vector, f32[1,512]{1,0:T(1,128)} %get-tuple-element.19.row.direction, f32[2,1,2048]{2,1,0:T(1,128)} %get-tuple-element.20.lift, ...), custom_call_target="tpu_custom_call" | custom-call | tf_op jit(solution)/shard_map/last/pallas_call | solution.py:229
Async XLA Ops:
  15.1 24.6 %all-to-all-start = ((f32[128,1,512]{2,1,0:T(1,128)}), f32[128,1,512]{2,1,0:T(1,128)S(1)}, u32[]{:S(2)}, u32[]{:S(2)}) async-start(f32[128,1,512]{2,1,0:T(1,128)} %copy.12), calls=%async_computation | async-start | bytes 524288 | tf_op jit(solution)/shard_map/all_to_all | solution.py:180
  68.2 23.3 %all-to-all-start.2 = ((f32[128,1,128]{2,1,0:T(1,128)}), f32[128,1,128]{2,1,0:T(1,128)S(1)}, u32[]{:S(2)}, u32[]{:S(2)}) async-start(f32[128,1,128]{2,1,0:T(1,128)} %bitcast.21), calls=%async_computation.2 | async-start | bytes 131072 | tf_op jit(solution)/shard_map/all_to_all | solution.py:180
  91.5 0.6 copy-start

commit v2 on v1

v2 whole, which is shorter than its diff:
```python
import jax
import jax.numpy as jnp
from jax import lax
from jax.experimental import pallas as pl
from jax.experimental.pallas import tpu as pltpu
from jax.sharding import PartitionSpec as P

BOTH = ("grp", "scen")
BLOCK = 256
LANES = 128
NT = (((1,), (1,)), ((), ()))
NN = (((1,), (0,)), ((), ()))
TN = (((0,), (0,)), ((), ()))
MIB = 1024 * 1024
SMEM_SPEC = pl.BlockSpec(memory_space=pltpu.SMEM)
VMEM_SPEC = pl.BlockSpec(memory_space=pltpu.VMEM)
HBM_SPEC = pl.BlockSpec(memory_space=pltpu.HBM)


def mul(a, b, dims):
    return lax.dot_general(a, b, dims, preferred_element_type=jnp.float32)


def thirds(value):
    high = value.astype(jnp.bfloat16).astype(jnp.float32)
    rest = value - high
    middle = rest.astype(jnp.bfloat16).astype(jnp.float32)
    return high, middle, rest - middle


def pieces(row):
    width = row.shape[1]
    ids = lax.broadcasted_iota(jnp.int32, (8, width), 0)
    high, middle, low = (jnp.broadcast_to(part, (8, width)) for part in thirds(row))
    out = jnp.where(ids == 0, high, jnp.where(ids == 1, middle, jnp.where(ids == 2, low, 0.0)))
    return out.astype(jnp.bfloat16)


def total(rows):
    return jnp.sum(rows, axis=0, keepdims=True)


def folded(row):
    return jnp.concatenate([row[:, i : i + LANES] for i in range(0, row.shape[1], LANES)], axis=0)


def unfolded(tile):
    return jnp.concatenate([tile[i : i + 1] for i in range(tile.shape[0])], axis=1)


def spread(row, out):
    out[...] = jnp.broadcast_to(folded(row)[None], out.shape)


def gathered(parts):
    return unfolded(jnp.sum(parts[...], axis=0))


def block_copy(s, i, linv, factor, sems):
    where = (s, pl.ds(i * BLOCK, BLOCK), pl.ds(0, (i + 1) * BLOCK))
    return pltpu.make_async_copy(linv.at[where], factor.at[where], sems.at[s, i])


def rows_copy(s, i, source, target, sems):
    where = (s, pl.ds(i * BLOCK, BLOCK))
    return pltpu.make_async_copy(source.at[where], target.at[where], sems.at[s, i])


def block_of(factor, s, i):
    return factor[s, pl.ds(i * BLOCK, BLOCK), pl.ds(0, (i + 1) * BLOCK)]


def kept_rows(columns, s, i, limit):
    part = columns[s, pl.ds(i * BLOCK, BLOCK)]
    ids = i * BLOCK + lax.broadcasted_iota(jnp.int32, part.shape, 0)
    return jnp.where(ids < limit, part, jnp.zeros_like(part))


def first_kernel(
    owner_in, weights_in, active_in, right_in, linv, link, lift_out, cross_out, scale_out,
    owner, weights, active, right, acc, factor, columns, small_sems, sems, link_sems,
):
    count, rows, width = columns.shape
    small = [
        pltpu.make_async_copy(a, b, small_sems.at[i])
        for i, (a, b) in enumerate([(right_in, right), (owner_in, owner), (weights_in, weights), (active_in, active)])
    ]
    for copy in small:
        copy.start()
    steps = [(0, (7,)), (0, (6, 5)), (0, (4, 3, 2, 1, 0)), (1, (7,)), (1, (6, 5)), (1, (4, 3)), (1, (2, 1, 0))]
    for s, group in steps:
        for i in group:
            block_copy(s, i, linv, factor, sems).start()
        for i in group:
            rows_copy(s, i, link, columns, link_sems).start()
    for copy in small:
        copy.wait()
    wide_right = right[...].astype(jnp.float32)
    wide = [jnp.broadcast_to(wide_right[s : s + 1], (8, rows)).astype(jnp.bfloat16) for s in range(count)]
    crosses = [jnp.zeros((8, width), jnp.float32) for s in range(count)]
    for s in range(count):
        acc[s] = jnp.zeros((8, rows), jnp.float32)

    def finish(step, lifted):
        s, group = step
        for i, row in zip(group, lifted):
            acc[s, :, pl.ds(0, (i + 1) * BLOCK)] += mul(row, block_of(factor, s, i), NN)
        for i in group:
            product = acc[s, pl.ds(0, 1), pl.ds(i * BLOCK, BLOCK)]
            crosses[s] = crosses[s] + mul(pieces(product), kept_rows(columns, s, i, active[s]), NN)

    before = None
    for step in steps:
        s, group = step
        for i in group:
            block_copy(s, i, linv, factor, sems).wait()
            rows_copy(s, i, link, columns, link_sems).wait()
        lifted = [mul(wide[s][:, : (i + 1) * BLOCK], block_of(factor, s, i), NT).astype(jnp.bfloat16) for i in group]
        if before:
            finish(*before)
        before = step, lifted
    finish(*before)
    cross = jnp.zeros((1, width), jnp.float32)
    for s in range(count):
        lift_out[s] = acc[s, pl.ds(0, 1), :]
        scale = weights[owner[s]]
        scale_out[s] = jnp.full((1, LANES), scale)
        cross = cross + scale * total(crosses[s])
    spread(cross, cross_out)


def gram_kernel(scale, active, linv, link, solved_out, gram_out, factor, columns, solved, sems, link_sems, out_sems):
    count, rows, width = columns.shape
    steps = [(0, (0, 1, 2, 3)), (0, (4, 5, 6, 7)), (1, (0, 1, 2, 3, 4, 5, 6, 7))]
    for s, group in steps:
        for i in group:
            rows_copy(s, i, link, columns, link_sems).start()
            block_copy(s, i, linv, factor, sems).start()
    for s, group in steps:
        for i in group:
            rows_copy(s, i, link, columns, link_sems).wait()
            block_copy(s, i, linv, factor, sems).wait()
        for i in group:
            columns[s, pl.ds(i * BLOCK, BLOCK)] = kept_rows(columns, s, i, active[s])
        for i in group:
            product = mul(block_of(factor, s, i), columns[s, pl.ds(0, (i + 1) * BLOCK)], NN)
            solved[s, pl.ds(i * BLOCK, BLOCK)] = product.astype(jnp.bfloat16)
        for i in group:
            rows_copy(s, i, solved, solved_out, out_sems).start()
    half = width // 2
    quads = []
    for top, left in ((0, 0), (0, half), (half, half)):
        quad = jnp.zeros((half, half), jnp.float32)
        for s in range(count):
            quad = quad + scale[s][:, :1] * mul(solved[s, :, pl.ds(top, half)], solved[s, :, pl.ds(left, half)], TN)
        quads.append(quad)
    gram = jnp.concatenate(
        [jnp.concatenate([quads[0], quads[1]], axis=1), jnp.concatenate([quads[1].T, quads[2]], axis=1)], axis=0
    )
    for i, part in enumerate(thirds(gram)):
        gram_out[i] = part.astype(jnp.bfloat16)
    for s in range(count):
        for i in range(rows // BLOCK):
            rows_copy(s, i, solved, solved_out, out_sems).wait()


def gram_times(row, gram):
    left = pieces(row)
    return total(mul(left, gram[0], NN) + mul(left, gram[1], NN) + mul(left, gram[2], NN))


def image_kernel(parts, rhs, gram, vector_out, image_out):
    vector = rhs[...] - gathered(parts)
    vector_out[...] = vector
    spread(gram_times(vector, gram), image_out)


def direction_kernel(parts, diag, vector_in, gram, after, direction_out, scalars_out, product_out):
    vector = vector_in[...]
    image = diag[...] * vector + gathered(parts)
    dot = lambda a, b: jnp.sum(a * b, axis=1, keepdims=True)
    norm = dot(vector, vector)
    alpha = norm / dot(vector, image)
    remain = vector - alpha * image
    norm_next = dot(remain, remain)
    direction = remain + (norm_next / norm) * vector
    direction_out[...] = direction
    wide = lambda value: jnp.broadcast_to(value, (1, LANES))
    scalars_out[pl.ds(0, 1)] = wide(alpha)
    scalars_out[pl.ds(1, 1)] = wide(norm_next)
    scalars_out[pl.ds(2, 1)] = wide(dot(direction * diag[...], direction))
    product_out[...] = jnp.broadcast_to(wide(dot(gram_times(direction, gram), direction))[None], product_out.shape)


def back_kernel(linv, solved_in, row, back_out, factor, solved, acc, sems, in_sems):
    count, rows, width = solved.shape
    blocks = rows // BLOCK
    groups = [tuple(range(blocks // 2)), tuple(range(blocks // 2, blocks))]
    for s in range(count):
        for group in groups:
            for i in group:
                rows_copy(s, i, solved_in, solved, in_sems).start()
                block_copy(s, i, linv, factor, sems).start()
    split = pieces(row[...])
    for s in range(count):
        acc[...] = jnp.zeros_like(acc)
        for group in groups:
            for i in group:
                rows_copy(s, i, solved_in, solved, in_sems).wait()
                block_copy(s, i, linv, factor, sems).wait()
            forward = [total(mul(split, solved[s, pl.ds(i * BLOCK, BLOCK)], NT)) for i in group]
            for i, part in zip(group, forward):
                acc[:, pl.ds(0, (i + 1) * BLOCK)] += mul(pieces(part), block_of(factor, s, i), NN)
        back_out[s] = total(acc[...])


def last_kernel(parts, scalars, vector, direction, lift, first, second, step_out, out):
    alpha = scalars[pl.ds(0, 1), pl.ds(0, 1)]
    norm = scalars[pl.ds(1, 1), pl.ds(0, 1)]
    bend = jnp.sum(parts[...], axis=0)[:, :1] + scalars[pl.ds(2, 1), pl.ds(0, 1)]
    beta = norm / bend
    step_out[...] = alpha * vector[...] + beta * direction[...]
    for s in range(out.shape[0]):
        out[pl.ds(s, 1)] = lift[s] - alpha * first[s] - beta * second[s]


def placed(array, spec):
    if spec is SMEM_SPEC:
        return array
    return pltpu.with_memory_space_constraint(array, spec.memory_space)


def kernel(fn, name, outs, scratch=(), specs=None, outs_specs=None, mib=8):
    def call(*args):
        return pl.pallas_call(
            fn,
            name=name,
            out_shape=outs,
            in_specs=specs or [VMEM_SPEC] * len(args),
            out_specs=outs_specs or jax.tree.map(lambda _: VMEM_SPEC, outs),
            scratch_shapes=scratch,
            compiler_params=pltpu.CompilerParams(vmem_limit_bytes=mib * MIB),
        )(*[placed(a, specs[i] if specs else VMEM_SPEC) for i, a in enumerate(args)])

    return call


def body(linv, link, residual_rows, active, owner, weights, first_diag, first_rhs):
    count, rows, width = link.shape
    blocks = rows // BLOCK
    devices = lax.axis_size(BOTH)
    f32 = lambda *dims: pltpu.VMEM(dims, jnp.float32)
    bf16 = lambda *dims: pltpu.VMEM(dims, jnp.bfloat16)
    folds = width // LANES

    def share(rows_of_all):
        return lax.all_to_all(rows_of_all, BOTH, 0, 0, tiled=True)

    diag = first_diag.reshape(1, width)
    rhs = first_rhs.reshape(1, width)
    block_sems = pltpu.SemaphoreType.DMA((count, blocks))
    factor = pltpu.VMEM((count, rows, rows), jnp.bfloat16)
    columns = pltpu.VMEM((count, rows, width), jnp.bfloat16)
    lift, cross, scale = kernel(
        first_kernel,
        "first",
        (f32(count, 1, rows), f32(devices, folds, LANES), f32(count, 1, LANES)),
        specs=[HBM_SPEC] * 6,
        scratch=[
            pltpu.SMEM((count,), jnp.int32),
            pltpu.SMEM(weights.shape, jnp.float32),
            pltpu.SMEM((count,), jnp.int32),
            pltpu.VMEM((count, rows), jnp.bfloat16),
            pltpu.VMEM((count, 8, rows), jnp.float32),
            factor,
            columns,
            pltpu.SemaphoreType.DMA((4,)),
            block_sems,
            block_sems,
        ],
        mib=40,
    )(owner, weights, active, residual_rows, linv, link)
    cross_parts = share(cross)
    solved, gram = kernel(
        gram_kernel,
        "gram",
        (pltpu.HBM((count, rows, width), jnp.bfloat16), bf16(3, width, width)),
        specs=[VMEM_SPEC, SMEM_SPEC, HBM_SPEC, HBM_SPEC],
        outs_specs=(HBM_SPEC, VMEM_SPEC),
        scratch=[factor, columns, columns, block_sems, block_sems, block_sems],
        mib=44,
    )(scale, active, linv, link)
    vector, image = kernel(image_kernel, "image", (f32(1, width), f32(devices, folds, LANES)))(cross_parts, rhs, gram)
    image_parts = share(image)

    def back(row, name):
        return kernel(
            back_kernel,
            name,
            f32(count, 1, rows),
            specs=[HBM_SPEC, HBM_SPEC, VMEM_SPEC],
            scratch=[factor, columns, pltpu.VMEM((8, rows), jnp.float32), block_sems, block_sems],
            mib=40,
        )(linv, solved, row)

    first = back(vector, "back_first")
    direction, scalars, product = kernel(direction_kernel, "direction", (f32(1, width), f32(3, LANES), f32(devices, 1, LANES)))(
        image_parts, diag, vector, gram, first
    )
    product_parts = share(product)
    second = back(direction, "back_second")
    step, out = kernel(
        last_kernel, "last", (jax.ShapeDtypeStruct((1, width), jnp.float32), jax.ShapeDtypeStruct((count, rows), jnp.float32))
    )(product_parts, scalars, vector, direction, lift, first, second)
    return step.reshape(width), out


def solution(mesh):
    placed = (
        P(BOTH, None, None),
        P(BOTH, None, None),
        P(BOTH, None),
        P(BOTH),
        P(BOTH),
        P(),
        P(),
        P(),
    )
    return jax.shard_map(body, mesh=mesh, in_specs=placed, out_specs=(P(), P(BOTH, None)), check_vma=False)
```

time: 94.5 us -> 73 us (0.77)
  blocking collectives: 20.4 us -> 0 us
  Pallas kernels: 50.3 us -> 37.3 us
  starting transfers between devices: 15.8 us -> 26 us
  waiting for transfers between devices: 0.01 us -> 8.11 us
  local copies, waits for them, and re-layouts: 6.57 us -> 0.02 us
    all_to_all x1 -> x0, blocking collectives: 20.4 us -> none  [share(): return lax.all_to_all(rows_of_all, BOTH, 0, 0, tiled=True)]
    pallas_call x7, Pallas kernels: 50.3 us -> 37.3 us  [call(): pl.pallas_call(fn, name=name, out_shape=outs, in_specs=specs or [VMEM_SPE...]
    all_to_all x2 -> x3, starting transfers between devices: 15.8 us -> 26 us  [share(): return lax.all_to_all(rows_of_all, BOTH, 0, 0, tiled=True)]
    all_to_all x2 -> x3, waiting for transfers between devices: 0.01 us -> 8.11 us  [share(): return lax.all_to_all(rows_of_all, BOTH, 0, 0, tiled=True)]
    all_to_all x2 -> x0, local copies, waits for them, and re-layouts: 3.16 us -> none  [share(): return lax.all_to_all(rows_of_all, BOTH, 0, 0, tiled=True)]
    unnamed x4 -> x6, local copies, waits for them, and re-layouts: 2.09 us -> 0.02 us
    reshape x1 -> x0, local copies, waits for them, and re-layouts: 1.31 us -> none  [body(): right = residual_rows.reshape(count, 1, rows)]
  transfers between devices with their start and end apart: 2 -> 3, of which waited for: 0 -> 3; matrix products, arithmetic and copies ran while one was open for 0% -> 0% of each run, Pallas kernels for 34% -> 32%
where the time goes in v2:
time: 73 us; the launch traced here: 72.2 us
  Pallas kernels  37.3 us (51%)
  starting transfers between devices  26 us (36%)
  waiting for transfers between devices  8.11 us (11%)
    pallas_call x7, Pallas kernels, call(): pl.pallas_call(fn, name=name, out_shape=outs, in_specs=specs or [VMEM_SPE...  37.3 us
    all_to_all x3, starting transfers between devices, share(): return lax.all_to_all(rows_of_all, BOTH, 0, 0, tiled=True)  26 us
    all_to_all x3, waiting for transfers between devices, share(): return lax.all_to_all(rows_of_all, BOTH, 0, 0, tiled=True)  8.11 us
  transfers between devices with their start and end apart: 3, of which 3 were waited for; matrix products, arithmetic and copies ran while one was open for 0% of the time, Pallas kernels for 32%

profile of v2, /device:TPU:0, one launch (start us, length us, event | category | flops | bytes accessed | tf_op | source)
XLA Modules:
  0.0 72.2 jit_solution(5656950315438258014)
XLA Ops:
  0.6 0.0 copy-start
  0.6 11.0 %first.1 = (f32[2,1,2048]{2,1,0:T(1,128)S(1)}, f32[128,4,128]{2,1,0:T(4,128)}, f32[2,1,128]{2,1,0:T(1,128)S(1)}) custom-call(s32[2]{0:T(128)} %owner_in.1, f32[256]{0:T(256)} %weights_in.1, s32[2]{0:T(128)} %active.1, bf16[2,2048]{1,0:T(2,128)(2,1)} %right_in.1, bf16[2,2048,2048]{2,1,0:T(8,128)(2,1)} %linv.7, bf16[2,2048,512]{2,1,0:T(8,128)(2,1)} %link.3), custom_call_target="tpu_custom_call" | custom-call | tf_op jit(solution)/shard_map/first/pallas_call | solution.py:235
  11.7 11.2 %all-to-all-start = ((f32[128,4,128]{2,1,0:T(4,128)}), f32[128,4,128]{2,1,0:T(4,128)S(1)}, u32[]{:S(2)}, u32[]{:S(2)}) async-start(f32[128,4,128]{2,1,0:T(4,128)} %get-tuple-element.14), calls=%async_computation | async-start | bytes 524288 | tf_op jit(solution)/shard_map/all_to_all | solution.py:257
  22.9 0.0 copy-done
  22.9 0.0 copy-start.2
  22.9 10.7 %gram.1 = (bf16[2,2048,512]{2,1,0:T(8,128)(2,1)}, bf16[3,512,512]{2,1,0:T(8,128)(2,1)S(1)}) custom-call(f32[2,1,128]{2,1,0:T(1,128)S(1)} %get-tuple-element.15.scale, s32[2]{0:T(128)S(1)} %copy-done, bf16[2,2048,2048]{2,1,0:T(8,128)(2,1)} %linv.7, bf16[2,2048,512]{2,1,0:T(8,128)(2,1)} %link.3), custom_call_target="tpu_custom_call" | custom-call | tf_op jit(solution)/shard_map/gram/pallas_call | solution.py:235
  33.6 0.1 all-to-all-done.parts
  33.7 0.0 copy-done.2
  33.7 1.2 %image.1 = (f32[1,512]{1,0:T(1,128)S(1)}, f32[128,4,128]{2,1,0:T(4,128)}) custom-call(f32[128,4,128]{2,1,0:T(4,128)S(1)} %all-to-all-done.parts, f32[1,512]{1,0:T(1,128)S(1)} %bitcast.4, bf16[3,512,512]{2,1,0:T(8,128)(2,1)S(1)} %get-tuple-element.16.gram), custom_call_target="tpu_custom_call" | custom-call | tf_op jit(solution)/shard_map/image/pallas_call | solution.py:235
  34.9 9.8 %all-to-all-start.1 = ((f32[128,4,128]{2,1,0:T(4,128)}), f32[128,4,128]{2,1,0:T(4,128)S(1)}, u32[]{:S(2)}, u32[]{:S(2)}) async-start(f32[128,4,128]{2,1,0:T(4,128)} %get-tuple-element.17), calls=%async_computation.1 | async-start | bytes 524288 | tf_op jit(solution)/shard_map/all_to_all | solution.py:257
  44.8 0.0 copy-start.1
  44.8 6.1 %back_first.1.after.first = f32[2,1,2048]{2,1,0:T(1,128)S(1)} custom-call(bf16[2,2048,2048]{2,1,0:T(8,128)(2,1)} %linv.7, bf16[2,2048,512]{2,1,0:T(8,128)(2,1)} %get-tuple-element.19.solved_in, f32[1,512]{1,0:T(1,128)S(1)} %get-tuple-element.18.row.vector_in.vector), custom_call_target="tpu_custom_call" | custom-call | tf_op jit(solution)/shard_map/back_first/pallas_call | solution.py:235
  50.9 4.6 %all-to-all-done.1.parts = f32[128,4,128]{2,1,0:T(4,128)S(1)} async-done(((f32[128,4,128]{2,1,0:T(4,128)}), f32[128,4,128]{2,1,0:T(4,128)S(1)}, u32[]{:S(2)}, u32[]{:S(2)}) %all-to-all-start.1) | async-done | bytes 262176 | tf_op jit(solution)/shard_map/all_to_all | solution.py:257
  55.5 0.0 copy-done.1
  55.5 1.4 %direction.1 = (f32[1,512]{1,0:T(1,128)S(1)}, f32[3,128]{1,0:T(4,128)S(1)}, f32[128,1,128]{2,1,0:T(1,128)}) custom-call(f32[128,4,128]{2,1,0:T(4,128)S(1)} %all-to-all-done.1.parts, f32[1,512]{1,0:T(1,128)S(1)} %bitcast.3, f32[1,512]{1,0:T(1,128)S(1)} %get-tuple-element.18.row.vector_in.vector, bf16[3,512,512]{2,1,0:T(8,128)(2,1)S(1)} %get-tuple-element.16.gram, ...), custom_call_target="tpu_custom_call" | custom-call | tf_op jit(solution)/shard_map/direction/pallas_call | solution.py:235
  56.8 5.0 %all-to-all-start.2 = ((f32[128,1,128]{2,1,0:T(1,128)}), f32[128,1,128]{2,1,0:T(1,128)S(1)}, u32[]{:S(2)}, u32[]{:S(2)}) async-start(f32[128,1,128]{2,1,0:T(1,128)} %get-tuple-element.20), calls=%async_computation.2 | async-start | bytes 131072 | tf_op jit(solution)/shard_map/all_to_all | solution.py:257
  61.9 6.1 %back_second.1.second = f32[2,1,2048]{2,1,0:T(1,128)S(1)} custom-call(bf16[2,2048,2048]{2,1,0:T(8,128)(2,1)} %linv.7, bf16[2,2048,512]{2,1,0:T(8,128)(2,1)} %get-tuple-element.19.solved_in, f32[1,512]{1,0:T(1,128)S(1)} %get-tuple-element.22.row.direction), custom_call_target="tpu_custom_call" | custom-call | tf_op jit(solution)/shard_map/back_second/pallas_call | solution.py:235
  67.9 3.4 %all-to-all-done.2.parts = f32[128,1,128]{2,1,0:T(1,128)S(1)} async-done(((f32[128,1,128]{2,1,0:T(1,128)}), f32[128,1,128]{2,1,0:T(1,128)S(1)}, u32[]{:S(2)}, u32[]{:S(2)}) %all-to-all-start.2) | async-done | bytes 65568 | tf_op jit(solution)/shard_map/all_to_all | solution.py:257
  71.4 0.8 %last.1 = (f32[1,512]{1,0:T(1,128)}, f32[2,2048]{1,0:T(2,128)}) custom-call(f32[128,1,128]{2,1,0:T(1,128)S(1)} %all-to-all-done.2.parts, f32[3,128]{1,0:T(4,128)S(1)} %get-tuple-element.21.scalars, f32[1,512]{1,0:T(1,128)S(1)} %get-tuple-element.18.row.vector_in.vector, f32[1,512]{1,0:T(1,128)S(1)} %get-tuple-element.22.row.direction, ...), custom_call_target="tpu_custom_call" | custom-call | tf_op jit(solution)/shard_map/last/pallas_call | solution.py:235
Async XLA Ops:
  0.6 22.3 %copy-start = (s32[2]{0:T(128)S(1)}, s32[2]{0:T(128)}, u32[]{:S(2)}) copy-start(s32[2]{0:T(128)} %active.1) | copy-start | bytes 28
  11.7 22.0 %all-to-all-start = ((f32[128,4,128]{2,1,0:T(4,128)}), f32[128,4,128]{2,1,0:T(4,128)S(1)}, u32[]{:S(2)}, u32[]{:S(2)}) async-start(f32[128,4,128]{2,1,0:T(4,128)} %get-tuple-element.14), calls=%async_computation | async-start | bytes 524288 | tf_op jit(solution)/shard_map/all_to_all | solution.py:257
  22.9 10.9 %copy-start.2 = (f32[512]{0:T(512)S(1)}, f32[512]{0:T(512)}, u32[]{:S(2)}) copy-start(f32[512]{0:T(512)} %param.15) | copy-start | bytes 6148
  34.9 20.5 %all-to-all-start.1 = ((f32[128,4,128]{2,1,0:T(4,128)}), f32[128,4,128]{2,1,0:T(4,128)S(1)}, u32[]{:S(2)}, u32[]{:S(2)}) async-start(f32[128,4,128]{2,1,0:T(4,128)} %get-tuple-element.17), calls=%async_computation.1 | async-start | bytes 524288 | tf_op jit(solution)/shard_map/all_to_all | solution.py:257
  44.8 10.7 %copy-start.1 = (f32[512]{0:T(512)S(1)}, f32[512]{0:T(512)}, u32[]{:S(2)}) copy-start(f32[512]{0:T(512)} %param.14) | copy-start | bytes 6148
  56.8 14.5 %all-to-all-start.2 = ((f32[128,1,128]{2,1,0:T(1,128)}), f32[128,1,128]{2,1,0:T(1,128)S(1)}, u32[]{:S(2)}, u32[]{:S(2)}) async-start(f32[128,1,128]{2,1,0:T(1,128)} %get-tuple-element.20), calls=%async_computation.2 | async-start | bytes 131072 | tf_op jit(solution)/shard_map/all_to_all | solution.py:257

commit v3 on v2

v3 whole, which is shorter than its diff:
```python
import jax
import jax.numpy as jnp
from jax import lax
from jax.experimental import pallas as pl
from jax.experimental.pallas import tpu as pltpu
from jax.sharding import PartitionSpec as P

BOTH = ("grp", "scen")
BLOCK = 256
LANES = 128
NT = (((1,), (1,)), ((), ()))
NN = (((1,), (0,)), ((), ()))
TN = (((0,), (0,)), ((), ()))
MIB = 1024 * 1024
STEPS = ((0, (0, 1)), (0, (2, 3)), (0, (4, 5)), (0, (6, 7)), (1, (0, 1, 2, 3)), (1, (4, 5)), (1, (6, 7)))
SMEM_SPEC = pl.BlockSpec(memory_space=pltpu.SMEM)
VMEM_SPEC = pl.BlockSpec(memory_space=pltpu.VMEM)
HBM_SPEC = pl.BlockSpec(memory_space=pltpu.HBM)


def mul(a, b, dims):
    return lax.dot_general(a, b, dims, preferred_element_type=jnp.float32)


def thirds(value):
    high = value.astype(jnp.bfloat16).astype(jnp.float32)
    rest = value - high
    middle = rest.astype(jnp.bfloat16).astype(jnp.float32)
    return high, middle, rest - middle


def pieces(row):
    width = row.shape[1]
    ids = lax.broadcasted_iota(jnp.int32, (8, width), 0)
    high, middle, low = (jnp.broadcast_to(part, (8, width)) for part in thirds(row))
    out = jnp.where(ids == 0, high, jnp.where(ids == 1, middle, jnp.where(ids == 2, low, 0.0)))
    return out.astype(jnp.bfloat16)


def total(rows):
    return jnp.sum(rows, axis=0, keepdims=True)


def folded(row):
    return jnp.concatenate([row[:, i : i + LANES] for i in range(0, row.shape[1], LANES)], axis=0)


def unfolded(tile):
    return jnp.concatenate([tile[i : i + 1] for i in range(tile.shape[0])], axis=1)


def spread(row, out):
    out[...] = jnp.broadcast_to(folded(row)[None], out.shape)


def gathered(parts):
    return unfolded(jnp.sum(parts[...], axis=0))


def block_copy(s, i, linv, factor, sems):
    where = (s, pl.ds(i * BLOCK, BLOCK), pl.ds(0, (i + 1) * BLOCK))
    return pltpu.make_async_copy(linv.at[where], factor.at[where], sems.at[s, i])


def rows_copy(s, i, source, target, sems):
    where = (s, pl.ds(i * BLOCK, BLOCK))
    return pltpu.make_async_copy(source.at[where], target.at[where], sems.at[s, i])


def block_of(factor, s, i):
    return factor[s, pl.ds(i * BLOCK, BLOCK), pl.ds(0, (i + 1) * BLOCK)]


def kept_rows(columns, s, i, limit):
    part = columns[s, pl.ds(i * BLOCK, BLOCK)]
    ids = i * BLOCK + lax.broadcasted_iota(jnp.int32, part.shape, 0)
    return jnp.where(ids < limit, part, jnp.zeros_like(part))


def lift_rows(factor, s, i, wide):
    part = jnp.zeros((BLOCK, LANES), jnp.float32)
    for at in range(0, (i + 1) * BLOCK, LANES):
        tile = factor[s, pl.ds(i * BLOCK, BLOCK), pl.ds(at, LANES)].astype(jnp.float32)
        part = part + tile * wide[:, at : at + LANES]
    return jnp.sum(part, axis=1, keepdims=True)


def first_kernel(
    owner_in, weights_in, active_in, right_in, linv, link, lift_out, cross_out, scale_out, solved_out,
    owner, weights, active, right, factor, columns, solved, small_sems, sems, link_sems, out_sems,
):
    count, rows, width = columns.shape
    small = [
        pltpu.make_async_copy(a, b, small_sems.at[i])
        for i, (a, b) in enumerate([(right_in, right), (owner_in, owner), (weights_in, weights), (active_in, active)])
    ]
    for copy in small:
        copy.start()
    steps = STEPS
    for s, group in steps:
        for i in group:
            rows_copy(s, i, link, columns, link_sems).start()
            block_copy(s, i, linv, factor, sems).start()
    for copy in small:
        copy.wait()
    wide_right = right[...].astype(jnp.float32)
    crosses = [jnp.zeros((8, width), jnp.float32) for s in range(count)]

    def finish(step, lifted):
        s, group = step
        for i, column in zip(group, lifted):
            rounded = solved[s, pl.ds(i * BLOCK, BLOCK)].astype(jnp.float32) * column
            crosses[s] = crosses[s] + jnp.sum(rounded.reshape(BLOCK // 8, 8, width), axis=0)
            rows_copy(s, i, solved, solved_out, out_sems).start()

    before = None
    for step in steps:
        s, group = step
        for i in group:
            rows_copy(s, i, link, columns, link_sems).wait()
            block_copy(s, i, linv, factor, sems).wait()
        for i in group:
            columns[s, pl.ds(i * BLOCK, BLOCK)] = kept_rows(columns, s, i, active[s])
        lifted = []
        for i in group:
            product = mul(block_of(factor, s, i), columns[s, pl.ds(0, (i + 1) * BLOCK)], NN)
            solved[s, pl.ds(i * BLOCK, BLOCK)] = product.astype(jnp.bfloat16)
            column = lift_rows(factor, s, i, wide_right[s : s + 1]).astype(jnp.bfloat16).astype(jnp.float32)
            lifted.append(column)
            lift_out[s, :, pl.ds(i * BLOCK, BLOCK)] = jnp.broadcast_to(column, (BLOCK, LANES)).T[:1]
        if before:
            finish(*before)
        before = step, lifted
    finish(*before)
    cross = jnp.zeros((1, width), jnp.float32)
    for s in range(count):
        scale = weights[owner[s]]
        scale_out[s] = jnp.full((1, LANES), scale)
        cross = cross + scale * total(crosses[s])
    spread(cross, cross_out)
    for s, group in steps:
        for i in group:
            rows_copy(s, i, solved, solved_out, out_sems).wait()


def gram_kernel(scale, solved_in, gram_out, solved, sems):
    count, rows, width = solved.shape
    copies = [pltpu.make_async_copy(solved_in.at[s], solved.at[s], sems.at[s]) for s in range(count)]
    for copy in copies:
        copy.start()
    half = width // 2
    spots = ((0, 0), (0, half), (half, half))
    quads = [jnp.zeros((half, half), jnp.float32) for _ in spots]
    for s in range(count):
        copies[s].wait()
        for k, (top, left) in enumerate(spots):
            quads[k] = quads[k] + scale[s][:, :1] * mul(solved[s, :, pl.ds(top, half)], solved[s, :, pl.ds(left, half)], TN)
    gram = jnp.concatenate(
        [jnp.concatenate([quads[0], quads[1]], axis=1), jnp.concatenate([quads[1].T, quads[2]], axis=1)], axis=0
    )
    for i, part in enumerate(thirds(gram)):
        gram_out[i] = part.astype(jnp.bfloat16)


def gram_times(row, gram):
    left = pieces(row)
    return total(mul(left, gram[0], NN) + mul(left, gram[1], NN) + mul(left, gram[2], NN))


def image_kernel(parts, rhs, gram, vector_out, image_out):
    vector = rhs[...] - gathered(parts)
    vector_out[...] = vector
    spread(gram_times(vector, gram), image_out)


def direction_kernel(parts, diag, vector_in, gram, direction_out, scalars_out, product_out):
    vector = vector_in[...]
    image = diag[...] * vector + gathered(parts)
    dot = lambda a, b: jnp.sum(a * b, axis=1, keepdims=True)
    norm = dot(vector, vector)
    alpha = norm / dot(vector, image)
    remain = vector - alpha * image
    norm_next = dot(remain, remain)
    direction = remain + (norm_next / norm) * vector
    direction_out[...] = direction
    wide = lambda value: jnp.broadcast_to(value, (1, LANES))
    scalars_out[pl.ds(0, 1)] = wide(alpha)
    scalars_out[pl.ds(1, 1)] = wide(norm_next)
    scalars_out[pl.ds(2, 1)] = wide(dot(direction * diag[...], direction))
    product_out[...] = jnp.broadcast_to(wide(dot(gram_times(direction, gram), direction))[None], product_out.shape)


def back_kernel(linv, solved_in, lift, vector, direction, back_out, factor, solved, acc, sems, in_sems):
    count, rows, width = solved.shape
    blocks = rows // BLOCK
    groups = [tuple(range(blocks // 2)), tuple(range(blocks // 2, blocks))]
    for s in range(count):
        for group in groups:
            for i in group:
                rows_copy(s, i, solved_in, solved, in_sems).start()
                block_copy(s, i, linv, factor, sems).start()
    left = jnp.concatenate([pieces(vector[...]), pieces(direction[...])], axis=0)
    ids = lax.broadcasted_iota(jnp.int32, (8, BLOCK), 0)

    def stacked(products, row):
        first = [jnp.broadcast_to(part, (8, BLOCK)) for part in thirds(total(products[:8]))]
        second = [jnp.broadcast_to(part, (8, BLOCK)) for part in thirds(total(products[8:]))]
        out = jnp.broadcast_to(row, (8, BLOCK))
        for k, part in enumerate(first + second):
            out = jnp.where(ids == k + 1, part, out)
        return jnp.where(ids < 7, out, 0.0).astype(jnp.bfloat16)

    for s in range(count):
        acc[...] = jnp.zeros_like(acc)
        for group in groups:
            for i in group:
                rows_copy(s, i, solved_in, solved, in_sems).wait()
                block_copy(s, i, linv, factor, sems).wait()
            products = [mul(left, solved[s, pl.ds(i * BLOCK, BLOCK)], NT) for i in group]
            for i, product in zip(group, products):
                row = lift[s, :, pl.ds(i * BLOCK, BLOCK)]
                acc[:, pl.ds(0, (i + 1) * BLOCK)] += mul(stacked(product, row), block_of(factor, s, i), NN)
        back_out[s] = acc[...]


def last_kernel(parts, scalars, vector, direction, back, step_out, out):
    alpha = scalars[pl.ds(0, 1), pl.ds(0, 1)]
    norm = scalars[pl.ds(1, 1), pl.ds(0, 1)]
    bend = jnp.sum(parts[...], axis=0)[:, :1] + scalars[pl.ds(2, 1), pl.ds(0, 1)]
    beta = norm / bend
    step_out[...] = alpha * vector[...] + beta * direction[...]
    for s in range(out.shape[0]):
        rows = back[s]
        out[pl.ds(s, 1)] = rows[0:1] - alpha * total(rows[1:4]) - beta * total(rows[4:7])


def placed(array, spec):
    if spec is SMEM_SPEC:
        return array
    return pltpu.with_memory_space_constraint(array, spec.memory_space)


def kernel(fn, name, outs, scratch=(), specs=None, outs_specs=None, mib=8):
    def call(*args):
        return pl.pallas_call(
            fn,
            name=name,
            out_shape=outs,
            in_specs=specs or [VMEM_SPEC] * len(args),
            out_specs=outs_specs or jax.tree.map(lambda _: VMEM_SPEC, outs),
            scratch_shapes=scratch,
            compiler_params=pltpu.CompilerParams(vmem_limit_bytes=mib * MIB),
        )(*[placed(a, specs[i] if specs else VMEM_SPEC) for i, a in enumerate(args)])

    return call


def body(linv, link, residual_rows, active, owner, weights, first_diag, first_rhs):
    count, rows, width = link.shape
    blocks = rows // BLOCK
    devices = lax.axis_size(BOTH)
    f32 = lambda *dims: pltpu.VMEM(dims, jnp.float32)
    bf16 = lambda *dims: pltpu.VMEM(dims, jnp.bfloat16)
    folds = width // LANES

    def share(rows_of_all):
        return lax.all_to_all(rows_of_all, BOTH, 0, 0, tiled=True)

    diag = first_diag.reshape(1, width)
    rhs = first_rhs.reshape(1, width)
    block_sems = pltpu.SemaphoreType.DMA((count, blocks))
    factor = pltpu.VMEM((count, rows, rows), jnp.bfloat16)
    columns = pltpu.VMEM((count, rows, width), jnp.bfloat16)
    lift, cross, scale, solved = kernel(
        first_kernel,
        "first",
        (
            f32(count, 1, rows),
            f32(devices, folds, LANES),
            f32(count, 1, LANES),
            pltpu.HBM((count, rows, width), jnp.bfloat16),
        ),
        specs=[HBM_SPEC] * 6,
        outs_specs=(VMEM_SPEC, VMEM_SPEC, VMEM_SPEC, HBM_SPEC),
        scratch=[
            pltpu.SMEM((count,), jnp.int32),
            pltpu.SMEM(weights.shape, jnp.float32),
            pltpu.SMEM((count,), jnp.int32),
            pltpu.VMEM((count, rows), jnp.bfloat16),
            factor,
            columns,
            columns,
            pltpu.SemaphoreType.DMA((4,)),
            block_sems,
            block_sems,
            block_sems,
        ],
        mib=44,
    )(owner, weights, active, residual_rows, linv, link)
    cross_parts = share(cross)
    gram = kernel(
        gram_kernel,
        "gram",
        bf16(3, width, width),
        specs=[VMEM_SPEC, HBM_SPEC],
        scratch=[columns, pltpu.SemaphoreType.DMA((count,))],
        mib=24,
    )(scale, solved)
    vector, image = kernel(image_kernel, "image", (f32(1, width), f32(devices, folds, LANES)))(cross_parts, rhs, gram)
    image_parts = share(image)
    direction, scalars, product = kernel(direction_kernel, "direction", (f32(1, width), f32(3, LANES), f32(devices, 1, LANES)))(
        image_parts, diag, vector, gram
    )
    product_parts = share(product)
    back = kernel(
        back_kernel,
        "back",
        f32(count, 8, rows),
        specs=[HBM_SPEC, HBM_SPEC, VMEM_SPEC, VMEM_SPEC, VMEM_SPEC],
        scratch=[factor, columns, pltpu.VMEM((8, rows), jnp.float32), block_sems, block_sems],
        mib=40,
    )(linv, solved, lift, vector, direction)
    step, out = kernel(
        last_kernel, "last", (jax.ShapeDtypeStruct((1, width), jnp.float32), jax.ShapeDtypeStruct((count, rows), jnp.float32))
    )(product_parts, scalars, vector, direction, back)
    return step.reshape(width), out


def solution(mesh):
    placed = (
        P(BOTH, None, None),
        P(BOTH, None, None),
        P(BOTH, None),
        P(BOTH),
        P(BOTH),
        P(),
        P(),
        P(),
    )
    return jax.shard_map(body, mesh=mesh, in_specs=placed, out_specs=(P(), P(BOTH, None)), check_vma=False)
```

time: 73 us -> 68.6 us (0.940)
  blocking collectives: 0 us -> 15.2 us
  Pallas kernels: 37.3 us -> 26 us
  starting transfers between devices: 26 us -> 15.8 us
  waiting for transfers between devices: 8.11 us -> 10.1 us
    all_to_all x0 -> x1, blocking collectives: none -> 15.2 us  [share(): return lax.all_to_all(rows_of_all, BOTH, 0, 0, tiled=True)]
    pallas_call x7 -> x6, Pallas kernels: 37.3 us -> 26 us  [call(): pl.pallas_call(fn, name=name, out_shape=outs, in_specs=specs or [VMEM_SPE...]
    all_to_all x3 -> x2, starting transfers between devices: 26 us -> 15.8 us  [share(): return lax.all_to_all(rows_of_all, BOTH, 0, 0, tiled=True)]
    all_to_all x3 -> x2, waiting for transfers between devices: 8.11 us -> 10.1 us  [share(): return lax.all_to_all(rows_of_all, BOTH, 0, 0, tiled=True)]
  transfers between devices with their start and end apart: 3 -> 2, of which waited for: 3 -> 2; matrix products, arithmetic and copies ran while one was open for 0% -> 0% of each run, Pallas kernels for 32% -> 15%
where the time goes in v3:
time: 68.6 us; the launch traced here: 67.8 us
  Pallas kernels  26 us (38%)
  starting transfers between devices  15.8 us (23%)
  blocking collectives  15.2 us (22%)
  waiting for transfers between devices  10.1 us (15%)
  between operations  0.7 us (1%)
    pallas_call x6, Pallas kernels, call(): pl.pallas_call(fn, name=name, out_shape=outs, in_specs=specs or [VMEM_SPE...  26 us
    all_to_all x2, starting transfers between devices, share(): return lax.all_to_all(rows_of_all, BOTH, 0, 0, tiled=True)  15.8 us
    all_to_all x1, blocking collectives, share(): return lax.all_to_all(rows_of_all, BOTH, 0, 0, tiled=True)  15.2 us
    all_to_all x2, waiting for transfers between devices, share(): return lax.all_to_all(rows_of_all, BOTH, 0, 0, tiled=True)  10.1 us
  transfers between devices with their start and end apart: 2, of which 2 were waited for; matrix products, arithmetic and copies ran while one was open for 0% of the time, Pallas kernels for 15%

profile of v3, /device:TPU:0, one launch (start us, length us, event | category | flops | bytes accessed | tf_op | source)
XLA Modules:
  0.0 67.8 jit_solution(17216814057688978604)
XLA Ops:
  0.6 13.0 %first.1 = (f32[2,1,2048]{2,1,0:T(1,128)S(1)}, f32[128,4,128]{2,1,0:T(4,128)}, f32[2,1,128]{2,1,0:T(1,128)S(1)}, bf16[2,2048,512]{2,1,0:T(8,128)(2,1)}) custom-call(s32[2]{0:T(128)} %owner_in.1, f32[256]{0:T(256)} %weights_in.1, s32[2]{0:T(128)} %active_in.1, bf16[2,2048]{1,0:T(2,128)(2,1)} %right_in.1, bf16[2,2048,2048]{2,1,0:T(8,128)(2,1)} %linv.3, ...), custom_call_target="tpu_custom_call" | custom-call | tf_op jit(solution)/shard_map/first/pallas_call | solution.py:245
  13.7 0.0 copy-start.1
  13.7 11.2 %all-to-all-start = ((f32[128,4,128]{2,1,0:T(4,128)}), f32[128,4,128]{2,1,0:T(4,128)S(1)}, u32[]{:S(2)}, u32[]{:S(2)}) async-start(f32[128,4,128]{2,1,0:T(4,128)} %get-tuple-element.13), calls=%async_computation | async-start | bytes 524288 | tf_op jit(solution)/shard_map/all_to_all | solution.py:267
  24.9 0.0 copy-start
  24.9 4.2 %gram.1 = bf16[3,512,512]{2,1,0:T(8,128)(2,1)S(1)} custom-call(f32[2,1,128]{2,1,0:T(1,128)S(1)} %get-tuple-element.14.scale, bf16[2,2048,512]{2,1,0:T(8,128)(2,1)} %get-tuple-element.15.solved_in), custom_call_target="tpu_custom_call" | custom-call | tf_op jit(solution)/shard_map/gram/pallas_call | solution.py:245
  29.1 6.6 %all-to-all-done.parts = f32[128,4,128]{2,1,0:T(4,128)S(1)} async-done(((f32[128,4,128]{2,1,0:T(4,128)}), f32[128,4,128]{2,1,0:T(4,128)S(1)}, u32[]{:S(2)}, u32[]{:S(2)}) %all-to-all-start) | async-done | bytes 262176 | tf_op jit(solution)/shard_map/all_to_all | solution.py:267
  35.7 0.0 copy-done.1
  35.7 0.5 image.1
  36.2 15.2 %all_to_all.15.parts = f32[128,4,128]{2,1,0:T(4,128)S(1)} all-to-all(f32[128,4,128]{2,1,0:T(4,128)S(1)} %get-tuple-element.16), channel_id=1, replica_groups=mesh['grp'=8,'scen'=16] {'grp','scen'}, dimensions={0} | all-to-all | bytes 524288 | tf_op jit(solution)/shard_map/all_to_all | solution.py:267
  51.5 0.0 copy-done
  51.5 1.4 %direction.1 = (f32[1,512]{1,0:T(1,128)S(1)}, f32[3,128]{1,0:T(4,128)S(1)}, f32[128,1,128]{2,1,0:T(1,128)}) custom-call(f32[128,4,128]{2,1,0:T(4,128)S(1)} %all_to_all.15.parts, f32[1,512]{1,0:T(1,128)S(1)} %bitcast.3, f32[1,512]{1,0:T(1,128)S(1)} %get-tuple-element.17.vector_in.vector, bf16[3,512,512]{2,1,0:T(8,128)(2,1)S(1)} %gram.1), custom_call_target="tpu_custom_call" | custom-call | tf_op jit(solution)/shard_map/direction/pallas_call | solution.py:245
  52.8 4.6 %all-to-all-start.2 = ((f32[128,1,128]{2,1,0:T(1,128)}), f32[128,1,128]{2,1,0:T(1,128)S(1)}, u32[]{:S(2)}, u32[]{:S(2)}) async-start(f32[128,1,128]{2,1,0:T(1,128)} %get-tuple-element.18), calls=%async_computation.2 | async-start | bytes 131072 | tf_op jit(solution)/shard_map/all_to_all | solution.py:267
  57.4 6.1 %back.1 = f32[2,8,2048]{2,1,0:T(8,128)S(1)} custom-call(bf16[2,2048,2048]{2,1,0:T(8,128)(2,1)} %linv.3, bf16[2,2048,512]{2,1,0:T(8,128)(2,1)} %get-tuple-element.15.solved_in, f32[2,1,2048]{2,1,0:T(1,128)S(1)} %get-tuple-element.21.lift, f32[1,512]{1,0:T(1,128)S(1)} %get-tuple-element.17.vector_in.vector, f32[1,512]{1,0:T(1,128)S(1)} %get-tuple-element.20.direction), custom_call_target="tpu_custom_call" | custom-call | tf_op jit(solution)/shard_map/back/pallas_call | solution.py:245
  63.5 3.4 %all-to-all-done.2.parts = f32[128,1,128]{2,1,0:T(1,128)S(1)} async-done(((f32[128,1,128]{2,1,0:T(1,128)}), f32[128,1,128]{2,1,0:T(1,128)S(1)}, u32[]{:S(2)}, u32[]{:S(2)}) %all-to-all-start.2) | async-done | bytes 65568 | tf_op jit(solution)/shard_map/all_to_all | solution.py:267
  66.9 0.8 %last.1 = (f32[1,512]{1,0:T(1,128)}, f32[2,2048]{1,0:T(2,128)}) custom-call(f32[128,1,128]{2,1,0:T(1,128)S(1)} %all-to-all-done.2.parts, f32[3,128]{1,0:T(4,128)S(1)} %get-tuple-element.19.scalars, f32[1,512]{1,0:T(1,128)S(1)} %get-tuple-element.17.vector_in.vector, f32[1,512]{1,0:T(1,128)S(1)} %get-tuple-element.20.direction, f32[2,8,2048]{2,1,0:T(8,128)S(1)} %back.1), custom_call_target="tpu_custom_call" | custom-call | tf_op jit(solution)/shard_map/last/pallas_call | solution.py:245
Async XLA Ops:
  13.7 22.1 %copy-start.1 = (f32[512]{0:T(512)S(1)}, f32[512]{0:T(512)}, u32[]{:S(2)}) copy-start(f32[512]{0:T(512)} %param.15) | copy-start | bytes 6148
  13.7 22.0 %all-to-all-start = ((f32[128,4,128]{2,1,0:T(4,128)}), f32[128,4,128]{2,1,0:T(4,128)S(1)}, u32[]{:S(2)}, u32[]{:S(2)}) async-start(f32[128,4,128]{2,1,0:T(4,128)} %get-tuple-element.13), calls=%async_computation | async-start | bytes 524288 | tf_op jit(solution)/shard_map/all_to_all | solution.py:267
  24.9 26.6 %copy-start = (f32[512]{0:T(512)S(1)}, f32[512]{0:T(512)}, u32[]{:S(2)}) copy-start(f32[512]{0:T(512)} %param.14) | copy-start | bytes 6148
  52.8 14.1 %all-to-all-start.2 = ((f32[128,1,128]{2,1,0:T(1,128)}), f32[128,1,128]{2,1,0:T(1,128)S(1)}, u32[]{:S(2)}, u32[]{:S(2)}) async-start(f32[128,1,128]{2,1,0:T(1,128)} %get-tuple-element.18), calls=%async_computation.2 | async-start | bytes 131072 | tf_op jit(solution)/shard_map/all_to_all | solution.py:267

commit v4 on v3

--- a/solution.py
+++ b/solution.py
@@ -12,7 +12,8 @@
 NN = (((1,), (0,)), ((), ()))
 TN = (((0,), (0,)), ((), ()))
 MIB = 1024 * 1024
-STEPS = ((0, (0, 1)), (0, (2, 3)), (0, (4, 5)), (0, (6, 7)), (1, (0, 1, 2, 3)), (1, (4, 5)), (1, (6, 7)))
+STEPS = ((0, (0, 1)), (0, (2, 3, 4)), (0, (5, 6, 7)), (1, (0, 1, 2, 3)), (1, (4, 5, 6, 7)))
+LAG = 2
 SMEM_SPEC = pl.BlockSpec(memory_space=pltpu.SMEM)
 VMEM_SPEC = pl.BlockSpec(memory_space=pltpu.VMEM)
 HBM_SPEC = pl.BlockSpec(memory_space=pltpu.HBM)
@@ -83,6 +84,14 @@
         tile = factor[s, pl.ds(i * BLOCK, BLOCK), pl.ds(at, LANES)].astype(jnp.float32)
         part = part + tile * wide[:, at : at + LANES]
     return jnp.sum(part, axis=1, keepdims=True)
+
+
+def mask_rows(columns, s, i, limit):
+    own = pl.ds(i * BLOCK, BLOCK)
+    ids = i * BLOCK + lax.broadcasted_iota(jnp.int32, (BLOCK, LANES), 0)
+    keep = jnp.where(ids < limit, 1.0, 0.0).astype(jnp.bfloat16)
+    for at in range(0, columns.shape[2], LANES):
+        columns[s, own, pl.ds(at, LANES)] = columns[s, own, pl.ds(at, LANES)] * keep
 
 
 def first_kernel(
@@ -92,53 +101,59 @@
     count, rows, width = columns.shape
     small = [
         pltpu.make_async_copy(a, b, small_sems.at[i])
-        for i, (a, b) in enumerate([(right_in, right), (owner_in, owner), (weights_in, weights), (active_in, active)])
+        for i, (a, b) in enumerate([(active_in, active), (right_in, right), (owner_in, owner), (weights_in, weights)])
     ]
-    for copy in small:
+    for copy in small[:2]:
         copy.start()
-    steps = STEPS
-    for s, group in steps:
+    for n, (s, group) in enumerate(STEPS):
         for i in group:
             rows_copy(s, i, link, columns, link_sems).start()
             block_copy(s, i, linv, factor, sems).start()
-    for copy in small:
-        copy.wait()
-    wide_right = right[...].astype(jnp.float32)
+        if n == 0:
+            for copy in small[2:]:
+                copy.start()
+    wide_right = None
     crosses = [jnp.zeros((8, width), jnp.float32) for s in range(count)]
 
-    def finish(step, lifted):
-        s, group = step
-        for i, column in zip(group, lifted):
-            rounded = solved[s, pl.ds(i * BLOCK, BLOCK)].astype(jnp.float32) * column
-            crosses[s] = crosses[s] + jnp.sum(rounded.reshape(BLOCK // 8, 8, width), axis=0)
-            rows_copy(s, i, solved, solved_out, out_sems).start()
-
-    before = None
-    for step in steps:
-        s, group = step
+    def lift(s, i, product):
+        column = lift_rows(factor, s, i, wide_right[s : s + 1]).astype(jnp.bfloat16).astype(jnp.float32)
+        lift_out[s, :, pl.ds(i * BLOCK, BLOCK)] = jnp.broadcast_to(column, (BLOCK, LANES)).T[:1]
+        if product is None:
+            product = solved[s, pl.ds(i * BLOCK, BLOCK)].astype(jnp.float32)
+        crosses[s] = crosses[s] + jnp.sum((product * column).reshape(BLOCK // 8, 8, width), axis=0)
+
+    waiting = []
+    for n, (s, group) in enumerate(STEPS):
         for i in group:
             rows_copy(s, i, link, columns, link_sems).wait()
             block_copy(s, i, linv, factor, sems).wait()
-        for i in group:
-            columns[s, pl.ds(i * BLOCK, BLOCK)] = kept_rows(columns, s, i, active[s])
-        lifted = []
+        if n == 0:
+            small[0].wait()
+        if n == LAG:
+            small[1].wait()
+            wide_right = right[...].astype(jnp.float32)
+        for i in group:
+            mask_rows(columns, s, i, active[s])
         for i in group:
             product = mul(block_of(factor, s, i), columns[s, pl.ds(0, (i + 1) * BLOCK)], NN)
             solved[s, pl.ds(i * BLOCK, BLOCK)] = product.astype(jnp.bfloat16)
-            column = lift_rows(factor, s, i, wide_right[s : s + 1]).astype(jnp.bfloat16).astype(jnp.float32)
-            lifted.append(column)
-            lift_out[s, :, pl.ds(i * BLOCK, BLOCK)] = jnp.broadcast_to(column, (BLOCK, LANES)).T[:1]
-        if before:
-            finish(*before)
-        before = step, lifted
-    finish(*before)
+            rows_copy(s, i, solved, solved_out, out_sems).start()
+            if n < LAG:
+                waiting.append((s, i))
+            else:
+                lift(s, i, product)
+        if n == LAG:
+            for late in waiting:
+                lift(*late, None)
+    for copy in small[2:]:
+        copy.wait()
     cross = jnp.zeros((1, width), jnp.float32)
     for s in range(count):
         scale = weights[owner[s]]
         scale_out[s] = jnp.full((1, LANES), scale)
         cross = cross + scale * total(crosses[s])
     spread(cross, cross_out)
-    for s, group in steps:
+    for s, group in STEPS:
         for i in group:
             rows_copy(s, i, solved, solved_out, out_sems).wait()
 

time: 68.6 us -> 66.8 us (0.974)
  Pallas kernels: 26 us -> 24.3 us
    pallas_call x6, Pallas kernels: 26 us -> 24.3 us  [call(): pl.pallas_call(fn, name=name, out_shape=outs, in_specs=specs or [VMEM_SPE...]
  transfers between devices with their start and end apart: 2 -> 2, of which waited for: 2 -> 2; matrix products, arithmetic and copies ran while one was open for 0% -> 0% of each run, Pallas kernels for 15% -> 16%
where the time goes in v4:
time: 66.8 us; the launch traced here: 66 us
  Pallas kernels  24.3 us (36%)
  starting transfers between devices  15.8 us (24%)
  blocking collectives  15.2 us (23%)
  waiting for transfers between devices  10.1 us (15%)
  between operations  0.7 us (1%)
    pallas_call x6, Pallas kernels, call(): pl.pallas_call(fn, name=name, out_shape=outs, in_specs=specs or [VMEM_SPE...  24.3 us
    all_to_all x2, starting transfers between devices, share(): return lax.all_to_all(rows_of_all, BOTH, 0, 0, tiled=True)  15.8 us
    all_to_all x1, blocking collectives, share(): return lax.all_to_all(rows_of_all, BOTH, 0, 0, tiled=True)  15.2 us
    all_to_all x2, waiting for transfers between devices, share(): return lax.all_to_all(rows_of_all, BOTH, 0, 0, tiled=True)  10.1 us
  transfers between devices with their start and end apart: 2, of which 2 were waited for; matrix products, arithmetic and copies ran while one was open for 0% of the time, Pallas kernels for 16%

profile of v4, /device:TPU:0, one launch (start us, length us, event | category | flops | bytes accessed | tf_op | source)
XLA Modules:
  0.0 66.0 jit_solution(15020556102999640569)
XLA Ops:
  0.6 11.3 %first.1 = (f32[2,1,2048]{2,1,0:T(1,128)S(1)}, f32[128,4,128]{2,1,0:T(4,128)}, f32[2,1,128]{2,1,0:T(1,128)S(1)}, bf16[2,2048,512]{2,1,0:T(8,128)(2,1)}) custom-call(s32[2]{0:T(128)} %owner_in.1, f32[256]{0:T(256)} %weights_in.1, s32[2]{0:T(128)} %active_in.1, bf16[2,2048]{1,0:T(2,128)(2,1)} %right_in.1, bf16[2,2048,2048]{2,1,0:T(8,128)(2,1)} %linv.3, ...), custom_call_target="tpu_custom_call" | custom-call | tf_op jit(solution)/shard_map/first/pallas_call | solution.py:260
  11.9 0.0 copy-start.1
  11.9 11.2 %all-to-all-start = ((f32[128,4,128]{2,1,0:T(4,128)}), f32[128,4,128]{2,1,0:T(4,128)S(1)}, u32[]{:S(2)}, u32[]{:S(2)}) async-start(f32[128,4,128]{2,1,0:T(4,128)} %get-tuple-element.13), calls=%async_computation | async-start | bytes 524288 | tf_op jit(solution)/shard_map/all_to_all | solution.py:282
  23.1 0.0 copy-start
  23.1 4.2 %gram.1 = bf16[3,512,512]{2,1,0:T(8,128)(2,1)S(1)} custom-call(f32[2,1,128]{2,1,0:T(1,128)S(1)} %get-tuple-element.14.scale, bf16[2,2048,512]{2,1,0:T(8,128)(2,1)} %get-tuple-element.15.solved_in), custom_call_target="tpu_custom_call" | custom-call | tf_op jit(solution)/shard_map/gram/pallas_call | solution.py:260
  27.3 6.6 %all-to-all-done.parts = f32[128,4,128]{2,1,0:T(4,128)S(1)} async-done(((f32[128,4,128]{2,1,0:T(4,128)}), f32[128,4,128]{2,1,0:T(4,128)S(1)}, u32[]{:S(2)}, u32[]{:S(2)}) %all-to-all-start) | async-done | bytes 262176 | tf_op jit(solution)/shard_map/all_to_all | solution.py:282
  34.0 0.0 copy-done.1
  34.0 0.5 image.1
  34.5 15.2 %all_to_all.15.parts = f32[128,4,128]{2,1,0:T(4,128)S(1)} all-to-all(f32[128,4,128]{2,1,0:T(4,128)S(1)} %get-tuple-element.16), channel_id=1, replica_groups=mesh['grp'=8,'scen'=16] {'grp','scen'}, dimensions={0} | all-to-all | bytes 524288 | tf_op jit(solution)/shard_map/all_to_all | solution.py:282
  49.7 0.0 copy-done
  49.7 1.4 %direction.1 = (f32[1,512]{1,0:T(1,128)S(1)}, f32[3,128]{1,0:T(4,128)S(1)}, f32[128,1,128]{2,1,0:T(1,128)}) custom-call(f32[128,4,128]{2,1,0:T(4,128)S(1)} %all_to_all.15.parts, f32[1,512]{1,0:T(1,128)S(1)} %bitcast.3, f32[1,512]{1,0:T(1,128)S(1)} %get-tuple-element.17.vector_in.vector, bf16[3,512,512]{2,1,0:T(8,128)(2,1)S(1)} %gram.1), custom_call_target="tpu_custom_call" | custom-call | tf_op jit(solution)/shard_map/direction/pallas_call | solution.py:260
  51.1 4.6 %all-to-all-start.2 = ((f32[128,1,128]{2,1,0:T(1,128)}), f32[128,1,128]{2,1,0:T(1,128)S(1)}, u32[]{:S(2)}, u32[]{:S(2)}) async-start(f32[128,1,128]{2,1,0:T(1,128)} %get-tuple-element.18), calls=%async_computation.2 | async-start | bytes 131072 | tf_op jit(solution)/shard_map/all_to_all | solution.py:282
  55.7 6.1 %back.1 = f32[2,8,2048]{2,1,0:T(8,128)S(1)} custom-call(bf16[2,2048,2048]{2,1,0:T(8,128)(2,1)} %linv.3, bf16[2,2048,512]{2,1,0:T(8,128)(2,1)} %get-tuple-element.15.solved_in, f32[2,1,2048]{2,1,0:T(1,128)S(1)} %get-tuple-element.21.lift, f32[1,512]{1,0:T(1,128)S(1)} %get-tuple-element.17.vector_in.vector, f32[1,512]{1,0:T(1,128)S(1)} %get-tuple-element.20.direction), custom_call_target="tpu_custom_call" | custom-call | tf_op jit(solution)/shard_map/back/pallas_call | solution.py:260
  61.8 3.4 %all-to-all-done.2.parts = f32[128,1,128]{2,1,0:T(1,128)S(1)} async-done(((f32[128,1,128]{2,1,0:T(1,128)}), f32[128,1,128]{2,1,0:T(1,128)S(1)}, u32[]{:S(2)}, u32[]{:S(2)}) %all-to-all-start.2) | async-done | bytes 65568 | tf_op jit(solution)/shard_map/all_to_all | solution.py:282
  65.2 0.8 %last.1 = (f32[1,512]{1,0:T(1,128)}, f32[2,2048]{1,0:T(2,128)}) custom-call(f32[128,1,128]{2,1,0:T(1,128)S(1)} %all-to-all-done.2.parts, f32[3,128]{1,0:T(4,128)S(1)} %get-tuple-element.19.scalars, f32[1,512]{1,0:T(1,128)S(1)} %get-tuple-element.17.vector_in.vector, f32[1,512]{1,0:T(1,128)S(1)} %get-tuple-element.20.direction, f32[2,8,2048]{2,1,0:T(8,128)S(1)} %back.1), custom_call_target="tpu_custom_call" | custom-call | tf_op jit(solution)/shard_map/last/pallas_call | solution.py:260
Async XLA Ops:
  11.9 22.1 %copy-start.1 = (f32[512]{0:T(512)S(1)}, f32[512]{0:T(512)}, u32[]{:S(2)}) copy-start(f32[512]{0:T(512)} %param.15) | copy-start | bytes 6148
  11.9 22.0 %all-to-all-start = ((f32[128,4,128]{2,1,0:T(4,128)}), f32[128,4,128]{2,1,0:T(4,128)S(1)}, u32[]{:S(2)}, u32[]{:S(2)}) async-start(f32[128,4,128]{2,1,0:T(4,128)} %get-tuple-element.13), calls=%async_computation | async-start | bytes 524288 | tf_op jit(solution)/shard_map/all_to_all | solution.py:282
  23.1 26.6 %copy-start = (f32[512]{0:T(512)S(1)}, f32[512]{0:T(512)}, u32[]{:S(2)}) copy-start(f32[512]{0:T(512)} %param.14) | copy-start | bytes 6148
  51.1 14.1 %all-to-all-start.2 = ((f32[128,1,128]{2,1,0:T(1,128)}), f32[128,1,128]{2,1,0:T(1,128)S(1)}, u32[]{:S(2)}, u32[]{:S(2)}) async-start(f32[128,1,128]{2,1,0:T(1,128)} %get-tuple-element.18), calls=%async_computation.2 | async-start | bytes 131072 | tf_op jit(solution)/shard_map/all_to_all | solution.py:282

commit v5 on v4

--- a/solution.py
+++ b/solution.py
@@ -13,7 +13,10 @@
 TN = (((0,), (0,)), ((), ()))
 MIB = 1024 * 1024
 STEPS = ((0, (0, 1)), (0, (2, 3, 4)), (0, (5, 6, 7)), (1, (0, 1, 2, 3)), (1, (4, 5, 6, 7)))
+BACK_STEPS = ((0, (0, 1, 2, 3)), (0, (4, 5, 6, 7)), (1, (0, 1, 2, 3)), (1, (4, 5)), (1, (6, 7)))
 LAG = 2
+DEPTH = 3
+NEAR = 4
 SMEM_SPEC = pl.BlockSpec(memory_space=pltpu.SMEM)
 VMEM_SPEC = pl.BlockSpec(memory_space=pltpu.VMEM)
 HBM_SPEC = pl.BlockSpec(memory_space=pltpu.HBM)
@@ -94,50 +97,64 @@
         columns[s, own, pl.ds(at, LANES)] = columns[s, own, pl.ds(at, LANES)] * keep
 
 
+def in_turn(steps, copies_of, depth, ready):
+    for n in range(min(depth, len(steps))):
+        for copy in copies_of(*steps[n]):
+            copy.start()
+    for n, step in enumerate(steps):
+        for copy in copies_of(*step):
+            copy.wait()
+        if n + depth < len(steps):
+            for copy in copies_of(*steps[n + depth]):
+                copy.start()
+        ready(n, *step)
+
+
 def first_kernel(
-    owner_in, weights_in, active_in, right_in, linv, link, lift_out, cross_out, scale_out, solved_out,
-    owner, weights, active, right, factor, columns, solved, small_sems, sems, link_sems, out_sems,
+    owner_in, weights_in, active_in, right_in, linv, link, lift_out, cross_out, scale_out, ahead_out, near_out,
+    owner, weights, active, right, factor, columns, ahead, small_sems, sems, link_sems, out_sems,
 ):
     count, rows, width = columns.shape
     small = [
         pltpu.make_async_copy(a, b, small_sems.at[i])
         for i, (a, b) in enumerate([(active_in, active), (right_in, right), (owner_in, owner), (weights_in, weights)])
     ]
-    for copy in small[:2]:
+    for copy in small:
         copy.start()
-    for n, (s, group) in enumerate(STEPS):
-        for i in group:
-            rows_copy(s, i, link, columns, link_sems).start()
-            block_copy(s, i, linv, factor, sems).start()
-        if n == 0:
-            for copy in small[2:]:
-                copy.start()
-    wide_right = None
     crosses = [jnp.zeros((8, width), jnp.float32) for s in range(count)]
+    waiting, sent, rights = [], [], []
+
+    def place(s, i):
+        at = s * rows + i * BLOCK
+        far = ahead.shape[0]
+        return (ahead, pl.ds(at, BLOCK)) if at < far else (near_out, pl.ds(at - far, BLOCK))
+
+    def copies_of(s, group):
+        return [rows_copy(s, i, link, columns, link_sems) for i in group] + [block_copy(s, i, linv, factor, sems) for i in group]
 
     def lift(s, i, product):
-        column = lift_rows(factor, s, i, wide_right[s : s + 1]).astype(jnp.bfloat16).astype(jnp.float32)
+        column = lift_rows(factor, s, i, rights[0][s : s + 1]).astype(jnp.bfloat16).astype(jnp.float32)
         lift_out[s, :, pl.ds(i * BLOCK, BLOCK)] = jnp.broadcast_to(column, (BLOCK, LANES)).T[:1]
         if product is None:
-            product = solved[s, pl.ds(i * BLOCK, BLOCK)].astype(jnp.float32)
+            solved, own = place(s, i)
+            product = solved[own].astype(jnp.float32)
         crosses[s] = crosses[s] + jnp.sum((product * column).reshape(BLOCK // 8, 8, width), axis=0)
 
-    waiting = []
-    for n, (s, group) in enumerate(STEPS):
-        for i in group:
-            rows_copy(s, i, link, columns, link_sems).wait()
-            block_copy(s, i, linv, factor, sems).wait()
+    def ready(n, s, group):
         if n == 0:
             small[0].wait()
         if n == LAG:
             small[1].wait()
-            wide_right = right[...].astype(jnp.float32)
+            rights.append(right[...].astype(jnp.float32))
         for i in group:
             mask_rows(columns, s, i, active[s])
         for i in group:
+            solved, own = place(s, i)
             product = mul(block_of(factor, s, i), columns[s, pl.ds(0, (i + 1) * BLOCK)], NN)
-            solved[s, pl.ds(i * BLOCK, BLOCK)] = product.astype(jnp.bfloat16)
-            rows_copy(s, i, solved, solved_out, out_sems).start()
+            solved[own] = product.astype(jnp.bfloat16)
+            if solved is ahead:
+                sent.append(pltpu.make_async_copy(ahead.at[own], ahead_out.at[own], out_sems.at[s, i]))
+                sent[-1].start()
             if n < LAG:
                 waiting.append((s, i))
             else:
@@ -145,6 +162,8 @@
         if n == LAG:
             for late in waiting:
                 lift(*late, None)
+
+    in_turn(STEPS, copies_of, DEPTH, ready)
     for copy in small[2:]:
         copy.wait()
     cross = jnp.zeros((1, width), jnp.float32)
@@ -153,28 +172,37 @@
         scale_out[s] = jnp.full((1, LANES), scale)
         cross = cross + scale * total(crosses[s])
     spread(cross, cross_out)
-    for s, group in STEPS:
-        for i in group:
-            rows_copy(s, i, solved, solved_out, out_sems).wait()
-
-
-def gram_kernel(scale, solved_in, gram_out, solved, sems):
-    count, rows, width = solved.shape
-    copies = [pltpu.make_async_copy(solved_in.at[s], solved.at[s], sems.at[s]) for s in range(count)]
-    for copy in copies:
+    for copy in sent:
+        copy.wait()
+
+
+def gram_kernel(scale, near, ahead_in, near_copy, gram_out, ahead, sems, out_sem):
+    width = ahead.shape[1]
+    rows = ahead.shape[0] - near.shape[0]
+    spans = (pl.ds(0, rows), pl.ds(rows, near.shape[0]))
+    coming = [pltpu.make_async_copy(ahead_in.at[span], ahead.at[span], sems.at[i]) for i, span in enumerate(spans)]
+    going = pltpu.make_async_copy(near, near_copy, out_sem)
+    for copy in coming:
         copy.start()
+    going.start()
     half = width // 2
     spots = ((0, 0), (0, half), (half, half))
-    quads = [jnp.zeros((half, half), jnp.float32) for _ in spots]
-    for s in range(count):
-        copies[s].wait()
-        for k, (top, left) in enumerate(spots):
-            quads[k] = quads[k] + scale[s][:, :1] * mul(solved[s, :, pl.ds(top, half)], solved[s, :, pl.ds(left, half)], TN)
+
+    def products(s, solved, span):
+        return [
+            scale[s][:, :1] * mul(solved[span, pl.ds(top, half)], solved[span, pl.ds(left, half)], TN) for top, left in spots
+        ]
+
+    quads = products(1, near, pl.ds(0, near.shape[0]))
+    for s in range(2):
+        coming[s].wait()
+        quads = [a + b for a, b in zip(quads, products(s, ahead, spans[s]))]
     gram = jnp.concatenate(
         [jnp.concatenate([quads[0], quads[1]], axis=1), jnp.concatenate([quads[1].T, quads[2]], axis=1)], axis=0
     )
     for i, part in enumerate(thirds(gram)):
         gram_out[i] = part.astype(jnp.bfloat16)
+    going.wait()
 
 
 def gram_times(row, gram):
@@ -205,17 +233,20 @@
     product_out[...] = jnp.broadcast_to(wide(dot(gram_times(direction, gram), direction))[None], product_out.shape)
 
 
-def back_kernel(linv, solved_in, lift, vector, direction, back_out, factor, solved, acc, sems, in_sems):
+def back_kernel(linv, ahead_in, near_in, lift, vector, direction, back_out, factor, solved, sems, in_sems):
     count, rows, width = solved.shape
-    blocks = rows // BLOCK
-    groups = [tuple(range(blocks // 2)), tuple(range(blocks // 2, blocks))]
-    for s in range(count):
-        for group in groups:
-            for i in group:
-                rows_copy(s, i, solved_in, solved, in_sems).start()
-                block_copy(s, i, linv, factor, sems).start()
     left = jnp.concatenate([pieces(vector[...]), pieces(direction[...])], axis=0)
     ids = lax.broadcasted_iota(jnp.int32, (8, BLOCK), 0)
+
+    def copies_of(s, group):
+        out = []
+        for i in group:
+            own = pl.ds(i * BLOCK, BLOCK)
+            at, far = s * rows + i * BLOCK, ahead_in.shape[0]
+            source = ahead_in.at[pl.ds(at, BLOCK)] if at < far else near_in.at[pl.ds(at - far, BLOCK)]
+            out.append(pltpu.make_async_copy(source, solved.at[s, own], in_sems.at[s, i]))
+            out.append(block_copy(s, i, linv, factor, sems))
+        return out
 
     def stacked(products, row):
         first = [jnp.broadcast_to(part, (8, BLOCK)) for part in thirds(total(products[:8]))]
@@ -225,17 +256,14 @@
             out = jnp.where(ids == k + 1, part, out)
         return jnp.where(ids < 7, out, 0.0).astype(jnp.bfloat16)
 
-    for s in range(count):
-        acc[...] = jnp.zeros_like(acc)
-        for group in groups:
-            for i in group:
-                rows_copy(s, i, solved_in, solved, in_sems).wait()
-                block_copy(s, i, linv, factor, sems).wait()
-            products = [mul(left, solved[s, pl.ds(i * BLOCK, BLOCK)], NT) for i in group]
-            for i, product in zip(group, products):
-                row = lift[s, :, pl.ds(i * BLOCK, BLOCK)]
-                acc[:, pl.ds(0, (i + 1) * BLOCK)] += mul(stacked(product, row), block_of(factor, s, i), NN)
-        back_out[s] = acc[...]
+    def ready(n, s, group):
+        products = [mul(left, solved[s, pl.ds(i * BLOCK, BLOCK)], NT) for i in group]
+        for i, product in zip(group, products):
+            row = lift[s, :, pl.ds(i * BLOCK, BLOCK)]
+            back_out[s, :, pl.ds(0, (i + 1) * BLOCK)] += mul(stacked(product, row), block_of(factor, s, i), NN)
+
+    back_out[...] = jnp.zeros_like(back_out)
+    in_turn(BACK_STEPS, copies_of, DEPTH, ready)
 
 
 def last_kernel(parts, scalars, vector, direction, back, step_out, out):
@@ -286,17 +314,21 @@
     block_sems = pltpu.SemaphoreType.DMA((count, blocks))
     factor = pltpu.VMEM((count, rows, rows), jnp.bfloat16)
     columns = pltpu.VMEM((count, rows, width), jnp.bfloat16)
-    lift, cross, scale, solved = kernel(
+    near_rows = NEAR * BLOCK
+    ahead_rows = count * rows - near_rows
+    ahead_solved = pltpu.VMEM((ahead_rows, width), jnp.bfloat16)
+    lift, cross, scale, ahead, near = kernel(
         first_kernel,
         "first",
         (
             f32(count, 1, rows),
             f32(devices, folds, LANES),
             f32(count, 1, LANES),
-            pltpu.HBM((count, rows, width), jnp.bfloat16),
+            pltpu.HBM((ahead_rows, width), jnp.bfloat16),
+            bf16(near_rows, width),
         ),
         specs=[HBM_SPEC] * 6,
-        outs_specs=(VMEM_SPEC, VMEM_SPEC, VMEM_SPEC, HBM_SPEC),
+        outs_specs=(VMEM_SPEC, VMEM_SPEC, VMEM_SPEC, HBM_SPEC, VMEM_SPEC),
         scratch=[
             pltpu.SMEM((count,), jnp.int32),
             pltpu.SMEM(weights.shape, jnp.float32),
@@ -304,23 +336,24 @@
             pltpu.VMEM((count, rows), jnp.bfloat16),
             factor,
             columns,
-            columns,
+            ahead_solved,
             pltpu.SemaphoreType.DMA((4,)),
             block_sems,
             block_sems,
             block_sems,
         ],
-        mib=44,
+        mib=40,
     )(owner, weights, active, residual_rows, linv, link)
     cross_parts = share(cross)
-    gram = kernel(
+    near_copy, gram = kernel(
         gram_kernel,
         "gram",
-        bf16(3, width, width),
-        specs=[VMEM_SPEC, HBM_SPEC],
-        scratch=[columns, pltpu.SemaphoreType.DMA((count,))],
+        (pltpu.HBM((near_rows, width), jnp.bfloat16), bf16(3, width, width)),
+        specs=[VMEM_SPEC, VMEM_SPEC, HBM_SPEC],
+        outs_specs=(HBM_SPEC, VMEM_SPEC),
+        scratch=[ahead_solved, pltpu.SemaphoreType.DMA((2,)), pltpu.SemaphoreType.DMA],
         mib=24,
-    )(scale, solved)
+    )(scale, near, ahead)
     vector, image = kernel(image_kernel, "image", (f32(1, width), f32(devices, folds, LANES)))(cross_parts, rhs, gram)
     image_parts = share(image)
     direction, scalars, product = kernel(direction_kernel, "direction", (f32(1, width), f32(3, LANES), f32(devices, 1, LANES)))(
@@ -331,10 +364,10 @@
         back_kernel,
         "back",
         f32(count, 8, rows),
-        specs=[HBM_SPEC, HBM_SPEC, VMEM_SPEC, VMEM_SPEC, VMEM_SPEC],
-        scratch=[factor, columns, pltpu.VMEM((8, rows), jnp.float32), block_sems, block_sems],
+        specs=[HBM_SPEC] * 3 + [VMEM_SPEC] * 3,
+        scratch=[factor, columns, block_sems, block_sems],
         mib=40,
-    )(linv, solved, lift, vector, direction)
+    )(linv, ahead, near_copy, lift, vector, direction)
     step, out = kernel(
         last_kernel, "last", (jax.ShapeDtypeStruct((1, width), jnp.float32), jax.ShapeDtypeStruct((count, rows), jnp.float32))
     )(product_parts, scalars, vector, direction, back)

time: 66.8 us -> 65.4 us (0.979)
  Pallas kernels: 24.3 us -> 22.5 us
    pallas_call x6, Pallas kernels: 24.3 us -> 22.5 us  [call(): pl.pallas_call(fn, name=name, out_shape=outs, in_specs=specs or [VMEM_SPE...]
where the time goes in v5:
time: 65.4 us; the launch traced here: 64.5 us
  Pallas kernels  22.5 us (34%)
  starting transfers between devices  15.8 us (24%)
  blocking collectives  15.2 us (23%)
  waiting for transfers between devices  10.2 us (16%)
  between operations  0.7 us (1%)
    pallas_call x6, Pallas kernels, call(): pl.pallas_call(fn, name=name, out_shape=outs, in_specs=specs or [VMEM_SPE...  22.5 us
    all_to_all x2, starting transfers between devices, share(): return lax.all_to_all(rows_of_all, BOTH, 0, 0, tiled=True)  15.8 us
    all_to_all x1, blocking collectives, share(): return lax.all_to_all(rows_of_all, BOTH, 0, 0, tiled=True)  15.2 us
    all_to_all x2, waiting for transfers between devices, share(): return lax.all_to_all(rows_of_all, BOTH, 0, 0, tiled=True)  10.2 us
  transfers between devices with their start and end apart: 2, of which 2 were waited for; matrix products, arithmetic and copies ran while one was open for 0% of the time, Pallas kernels for 16%

profile of v5, /device:TPU:0, one launch (start us, length us, event | category | flops | bytes accessed | tf_op | source)
XLA Modules:
  0.0 64.5 jit_solution(14704171138827043463)
XLA Ops:
  0.6 9.7 %first.1 = (f32[2,1,2048]{2,1,0:T(1,128)S(1)}, f32[128,4,128]{2,1,0:T(4,128)}, f32[2,1,128]{2,1,0:T(1,128)S(1)}, bf16[3072,512]{1,0:T(8,128)(2,1)}, bf16[1024,512]{1,0:T(8,128)(2,1)S(1)}) custom-call(s32[2]{0:T(128)} %owner_in.1, f32[256]{0:T(256)} %weights_in.1, s32[2]{0:T(128)} %active_in.1, bf16[2,2048]{1,0:T(2,128)(2,1)} %right_in.1, ...), custom_call_target="tpu_custom_call" | custom-call | tf_op jit(solution)/shard_map/first/pallas_call | solution.py:288
  10.4 0.0 copy-start.1
  10.4 0.0 copy-start
  10.4 11.2 %all-to-all-start = ((f32[128,4,128]{2,1,0:T(4,128)}), f32[128,4,128]{2,1,0:T(4,128)S(1)}, u32[]{:S(2)}, u32[]{:S(2)}) async-start(f32[128,4,128]{2,1,0:T(4,128)} %get-tuple-element.16), calls=%async_computation | async-start | bytes 524288 | tf_op jit(solution)/shard_map/all_to_all | solution.py:310
  21.6 4.1 %gram.1 = (bf16[1024,512]{1,0:T(8,128)(2,1)}, bf16[3,512,512]{2,1,0:T(8,128)(2,1)S(1)}) custom-call(f32[2,1,128]{2,1,0:T(1,128)S(1)} %get-tuple-element.17.scale, bf16[1024,512]{1,0:T(8,128)(2,1)S(1)} %get-tuple-element.18.near, bf16[3072,512]{1,0:T(8,128)(2,1)} %get-tuple-element.19.ahead_in), custom_call_target="tpu_custom_call" | custom-call | tf_op jit(solution)/shard_map/gram/pallas_call | solution.py:288
  25.7 6.8 %all-to-all-done.parts = f32[128,4,128]{2,1,0:T(4,128)S(1)} async-done(((f32[128,4,128]{2,1,0:T(4,128)}), f32[128,4,128]{2,1,0:T(4,128)S(1)}, u32[]{:S(2)}, u32[]{:S(2)}) %all-to-all-start) | async-done | bytes 262176 | tf_op jit(solution)/shard_map/all_to_all | solution.py:310
  32.4 0.0 copy-done.1
  32.4 0.5 image.1
  32.9 15.2 %all_to_all.15.parts = f32[128,4,128]{2,1,0:T(4,128)S(1)} all-to-all(f32[128,4,128]{2,1,0:T(4,128)S(1)} %get-tuple-element.21), channel_id=1, replica_groups=mesh['grp'=8,'scen'=16] {'grp','scen'}, dimensions={0} | all-to-all | bytes 524288 | tf_op jit(solution)/shard_map/all_to_all | solution.py:310
  48.2 0.0 copy-done
  48.2 1.4 %direction.1 = (f32[1,512]{1,0:T(1,128)S(1)}, f32[3,128]{1,0:T(4,128)S(1)}, f32[128,1,128]{2,1,0:T(1,128)}) custom-call(f32[128,4,128]{2,1,0:T(4,128)S(1)} %all_to_all.15.parts, f32[1,512]{1,0:T(1,128)S(1)} %bitcast.3, f32[1,512]{1,0:T(1,128)S(1)} %get-tuple-element.22.vector_in.vector, bf16[3,512,512]{2,1,0:T(8,128)(2,1)S(1)} %get-tuple-element.20.gram), custom_call_target="tpu_custom_call" | custom-call | tf_op jit(solution)/shard_map/direction/pallas_call | solution.py:288
  49.6 4.6 %all-to-all-start.2 = ((f32[128,1,128]{2,1,0:T(1,128)}), f32[128,1,128]{2,1,0:T(1,128)S(1)}, u32[]{:S(2)}, u32[]{:S(2)}) async-start(f32[128,1,128]{2,1,0:T(1,128)} %get-tuple-element.23), calls=%async_computation.2 | async-start | bytes 131072 | tf_op jit(solution)/shard_map/all_to_all | solution.py:310
  54.2 6.0 %back.1 = f32[2,8,2048]{2,1,0:T(8,128)S(1)} custom-call(bf16[2,2048,2048]{2,1,0:T(8,128)(2,1)} %linv.3, bf16[3072,512]{1,0:T(8,128)(2,1)} %get-tuple-element.19.ahead_in, bf16[1024,512]{1,0:T(8,128)(2,1)} %get-tuple-element.26.near_in, f32[2,1,2048]{2,1,0:T(1,128)S(1)} %get-tuple-element.27.lift, f32[1,512]{1,0:T(1,128)S(1)} %get-tuple-element.22.vector_in.vector, ...), custom_call_target="tpu_custom_call" | custom-call | tf_op jit(solution)/shard_map/back/pallas_call | solution.py:288
  60.2 3.5 %all-to-all-done.2.parts = f32[128,1,128]{2,1,0:T(1,128)S(1)} async-done(((f32[128,1,128]{2,1,0:T(1,128)}), f32[128,1,128]{2,1,0:T(1,128)S(1)}, u32[]{:S(2)}, u32[]{:S(2)}) %all-to-all-start.2) | async-done | bytes 65568 | tf_op jit(solution)/shard_map/all_to_all | solution.py:310
  63.7 0.8 %last.1 = (f32[1,512]{1,0:T(1,128)}, f32[2,2048]{1,0:T(2,128)}) custom-call(f32[128,1,128]{2,1,0:T(1,128)S(1)} %all-to-all-done.2.parts, f32[3,128]{1,0:T(4,128)S(1)} %get-tuple-element.24.scalars, f32[1,512]{1,0:T(1,128)S(1)} %get-tuple-element.22.vector_in.vector, f32[1,512]{1,0:T(1,128)S(1)} %get-tuple-element.25.direction, f32[2,8,2048]{2,1,0:T(8,128)S(1)} %back.1), custom_call_target="tpu_custom_call" | custom-call | tf_op jit(solution)/shard_map/last/pallas_call | solution.py:288
Async XLA Ops:
  10.4 22.1 %copy-start.1 = (f32[512]{0:T(512)S(1)}, f32[512]{0:T(512)}, u32[]{:S(2)}) copy-start(f32[512]{0:T(512)} %param.15) | copy-start | bytes 6148
  10.4 37.8 %copy-start = (f32[512]{0:T(512)S(1)}, f32[512]{0:T(512)}, u32[]{:S(2)}) copy-start(f32[512]{0:T(512)} %param.14) | copy-start | bytes 6148
  10.4 22.0 %all-to-all-start = ((f32[128,4,128]{2,1,0:T(4,128)}), f32[128,4,128]{2,1,0:T(4,128)S(1)}, u32[]{:S(2)}, u32[]{:S(2)}) async-start(f32[128,4,128]{2,1,0:T(4,128)} %get-tuple-element.16), calls=%async_computation | async-start | bytes 524288 | tf_op jit(solution)/shard_map/all_to_all | solution.py:310
  49.6 14.1 %all-to-all-start.2 = ((f32[128,1,128]{2,1,0:T(1,128)}), f32[128,1,128]{2,1,0:T(1,128)S(1)}, u32[]{:S(2)}, u32[]{:S(2)}) async-start(f32[128,1,128]{2,1,0:T(1,128)} %get-tuple-element.23), calls=%async_computation.2 | async-start | bytes 131072 | tf_op jit(solution)/shard_map/all_to_all | solution.py:310

commit v6 on v5

--- a/solution.py
+++ b/solution.py
@@ -12,10 +12,10 @@
 NN = (((1,), (0,)), ((), ()))
 TN = (((0,), (0,)), ((), ()))
 MIB = 1024 * 1024
-STEPS = ((0, (0, 1)), (0, (2, 3, 4)), (0, (5, 6, 7)), (1, (0, 1, 2, 3)), (1, (4, 5, 6, 7)))
+STEPS = ((0, (0, 1)), (0, (2, 3)), (0, (4, 5)), (0, (6, 7)), (1, (0, 1, 2, 3)), (1, (4, 5)), (1, (6,)), (1, (7,)))
 BACK_STEPS = ((0, (0, 1, 2, 3)), (0, (4, 5, 6, 7)), (1, (0, 1, 2, 3)), (1, (4, 5)), (1, (6, 7)))
 LAG = 2
-DEPTH = 3
+DEPTH = 4
 NEAR = 4
 SMEM_SPEC = pl.BlockSpec(memory_space=pltpu.SMEM)
 VMEM_SPEC = pl.BlockSpec(memory_space=pltpu.VMEM)

time: 65.4 us -> 65.3 us (level)
  no operation moved by 1% of the time
where the time goes in v6:
time: 65.3 us; the launch traced here: 64.5 us
  Pallas kernels  22.5 us (34%)
  starting transfers between devices  15.8 us (24%)
  blocking collectives  15.2 us (23%)
  waiting for transfers between devices  10.2 us (16%)
  between operations  0.7 us (1%)
    pallas_call x6, Pallas kernels, call(): pl.pallas_call(fn, name=name, out_shape=outs, in_specs=specs or [VMEM_SPE...  22.5 us
    all_to_all x2, starting transfers between devices, share(): return lax.all_to_all(rows_of_all, BOTH, 0, 0, tiled=True)  15.8 us
    all_to_all x1, blocking collectives, share(): return lax.all_to_all(rows_of_all, BOTH, 0, 0, tiled=True)  15.2 us
    all_to_all x2, waiting for transfers between devices, share(): return lax.all_to_all(rows_of_all, BOTH, 0, 0, tiled=True)  10.2 us
  transfers between devices with their start and end apart: 2, of which 2 were waited for; matrix products, arithmetic and copies ran while one was open for 0% of the time, Pallas kernels for 16%

profile of v6, /device:TPU:0, one launch (start us, length us, event | category | flops | bytes accessed | tf_op | source)
XLA Modules:
  0.0 64.5 jit_solution(4804091941325402846)
XLA Ops:
  0.6 9.7 %first.1 = (f32[2,1,2048]{2,1,0:T(1,128)S(1)}, f32[128,4,128]{2,1,0:T(4,128)}, f32[2,1,128]{2,1,0:T(1,128)S(1)}, bf16[3072,512]{1,0:T(8,128)(2,1)}, bf16[1024,512]{1,0:T(8,128)(2,1)S(1)}) custom-call(s32[2]{0:T(128)} %owner_in.1, f32[256]{0:T(256)} %weights_in.1, s32[2]{0:T(128)} %active_in.1, bf16[2,2048]{1,0:T(2,128)(2,1)} %right_in.1, ...), custom_call_target="tpu_custom_call" | custom-call | tf_op jit(solution)/shard_map/first/pallas_call | solution.py:288
  10.3 0.0 copy-start.1
  10.4 0.0 copy-start
  10.4 11.2 %all-to-all-start = ((f32[128,4,128]{2,1,0:T(4,128)}), f32[128,4,128]{2,1,0:T(4,128)S(1)}, u32[]{:S(2)}, u32[]{:S(2)}) async-start(f32[128,4,128]{2,1,0:T(4,128)} %get-tuple-element.16), calls=%async_computation | async-start | bytes 524288 | tf_op jit(solution)/shard_map/all_to_all | solution.py:310
  21.6 4.1 %gram.1 = (bf16[1024,512]{1,0:T(8,128)(2,1)}, bf16[3,512,512]{2,1,0:T(8,128)(2,1)S(1)}) custom-call(f32[2,1,128]{2,1,0:T(1,128)S(1)} %get-tuple-element.17.scale, bf16[1024,512]{1,0:T(8,128)(2,1)S(1)} %get-tuple-element.18.near, bf16[3072,512]{1,0:T(8,128)(2,1)} %get-tuple-element.19.ahead_in), custom_call_target="tpu_custom_call" | custom-call | tf_op jit(solution)/shard_map/gram/pallas_call | solution.py:288
  25.7 6.8 %all-to-all-done.parts = f32[128,4,128]{2,1,0:T(4,128)S(1)} async-done(((f32[128,4,128]{2,1,0:T(4,128)}), f32[128,4,128]{2,1,0:T(4,128)S(1)}, u32[]{:S(2)}, u32[]{:S(2)}) %all-to-all-start) | async-done | bytes 262176 | tf_op jit(solution)/shard_map/all_to_all | solution.py:310
  32.4 0.0 copy-done.1
  32.4 0.5 image.1
  32.9 15.2 %all_to_all.15.parts = f32[128,4,128]{2,1,0:T(4,128)S(1)} all-to-all(f32[128,4,128]{2,1,0:T(4,128)S(1)} %get-tuple-element.21), channel_id=1, replica_groups=mesh['grp'=8,'scen'=16] {'grp','scen'}, dimensions={0} | all-to-all | bytes 524288 | tf_op jit(solution)/shard_map/all_to_all | solution.py:310
  48.2 0.0 copy-done
  48.2 1.4 %direction.1 = (f32[1,512]{1,0:T(1,128)S(1)}, f32[3,128]{1,0:T(4,128)S(1)}, f32[128,1,128]{2,1,0:T(1,128)}) custom-call(f32[128,4,128]{2,1,0:T(4,128)S(1)} %all_to_all.15.parts, f32[1,512]{1,0:T(1,128)S(1)} %bitcast.3, f32[1,512]{1,0:T(1,128)S(1)} %get-tuple-element.22.vector_in.vector, bf16[3,512,512]{2,1,0:T(8,128)(2,1)S(1)} %get-tuple-element.20.gram), custom_call_target="tpu_custom_call" | custom-call | tf_op jit(solution)/shard_map/direction/pallas_call | solution.py:288
  49.5 4.6 %all-to-all-start.2 = ((f32[128,1,128]{2,1,0:T(1,128)}), f32[128,1,128]{2,1,0:T(1,128)S(1)}, u32[]{:S(2)}, u32[]{:S(2)}) async-start(f32[128,1,128]{2,1,0:T(1,128)} %get-tuple-element.23), calls=%async_computation.2 | async-start | bytes 131072 | tf_op jit(solution)/shard_map/all_to_all | solution.py:310
  54.1 6.0 %back.1 = f32[2,8,2048]{2,1,0:T(8,128)S(1)} custom-call(bf16[2,2048,2048]{2,1,0:T(8,128)(2,1)} %linv.3, bf16[3072,512]{1,0:T(8,128)(2,1)} %get-tuple-element.19.ahead_in, bf16[1024,512]{1,0:T(8,128)(2,1)} %get-tuple-element.26.near_in, f32[2,1,2048]{2,1,0:T(1,128)S(1)} %get-tuple-element.27.lift, f32[1,512]{1,0:T(1,128)S(1)} %get-tuple-element.22.vector_in.vector, ...), custom_call_target="tpu_custom_call" | custom-call | tf_op jit(solution)/shard_map/back/pallas_call | solution.py:288
  60.2 3.5 %all-to-all-done.2.parts = f32[128,1,128]{2,1,0:T(1,128)S(1)} async-done(((f32[128,1,128]{2,1,0:T(1,128)}), f32[128,1,128]{2,1,0:T(1,128)S(1)}, u32[]{:S(2)}, u32[]{:S(2)}) %all-to-all-start.2) | async-done | bytes 65568 | tf_op jit(solution)/shard_map/all_to_all | solution.py:310
  63.6 0.8 %last.1 = (f32[1,512]{1,0:T(1,128)}, f32[2,2048]{1,0:T(2,128)}) custom-call(f32[128,1,128]{2,1,0:T(1,128)S(1)} %all-to-all-done.2.parts, f32[3,128]{1,0:T(4,128)S(1)} %get-tuple-element.24.scalars, f32[1,512]{1,0:T(1,128)S(1)} %get-tuple-element.22.vector_in.vector, f32[1,512]{1,0:T(1,128)S(1)} %get-tuple-element.25.direction, f32[2,8,2048]{2,1,0:T(8,128)S(1)} %back.1), custom_call_target="tpu_custom_call" | custom-call | tf_op jit(solution)/shard_map/last/pallas_call | solution.py:288
Async XLA Ops:
  10.3 22.1 %copy-start.1 = (f32[512]{0:T(512)S(1)}, f32[512]{0:T(512)}, u32[]{:S(2)}) copy-start(f32[512]{0:T(512)} %param.15) | copy-start | bytes 6148
  10.4 37.8 %copy-start = (f32[512]{0:T(512)S(1)}, f32[512]{0:T(512)}, u32[]{:S(2)}) copy-start(f32[512]{0:T(512)} %param.14) | copy-start | bytes 6148
  10.4 22.0 %all-to-all-start = ((f32[128,4,128]{2,1,0:T(4,128)}), f32[128,4,128]{2,1,0:T(4,128)S(1)}, u32[]{:S(2)}, u32[]{:S(2)}) async-start(f32[128,4,128]{2,1,0:T(4,128)} %get-tuple-element.16), calls=%async_computation | async-start | bytes 524288 | tf_op jit(solution)/shard_map/all_to_all | solution.py:310
  49.5 14.1 %all-to-all-start.2 = ((f32[128,1,128]{2,1,0:T(1,128)}), f32[128,1,128]{2,1,0:T(1,128)S(1)}, u32[]{:S(2)}, u32[]{:S(2)}) async-start(f32[128,1,128]{2,1,0:T(1,128)} %get-tuple-element.23), calls=%async_computation.2 | async-start | bytes 131072 | tf_op jit(solution)/shard_map/all_to_all | solution.py:310
